TPU v7x, 512 devices: a whole 4x4x16 slice. The times are simulated.
512 devices in a mesh: gx: 32 (over x, y, core), gy: 16 (over z).
Axes of the slice: x: 4, y: 4, z: 16, core: 2. Of those that a mesh axis runs over, the one named last changes fastest.
Arguments:
- right_side: float32 [512, 256, 128], P('gx', 'gy'), may hold values from -24 to 24
- material: int32 [512, 256, 128], P('gx', 'gy'), may hold values from 0 to 15
- conductivity: float32 [16], replicated, may hold values from 0.2 to 5
Outputs:
- solution_field: float32 [512, 256, 128], P('gx', 'gy')
All inputs are finite; a program needn't handle non-finite values.
Results may differ from a plain program's by a relative error of at most 0.0001.
Values sent between devices are 32-bit elements; how exact they have to be, the bound alone decides.
A program may use at most 64 MiB of HBM per device.

v0:
```python
import jax
import jax.numpy as jnp
from jax import lax
from jax.sharding import PartitionSpec as P

CYCLES = 2
COARSE_SWEEPS = 6


OMEGA = 0.8


def extended(x, sides, width):
    for axis, dim in sides:
        devices, length = (lax.axis_size(axis), x.shape[dim])
        up = [(i, (i + 1) % devices) for i in range(devices - 1)]
        down = [(j, i) for i, j in up]
        last = lax.slice_in_dim(x, length - width, length, axis=dim)
        first = lax.slice_in_dim(x, 0, width, axis=dim)
        before = lax.ppermute(last, axis, up)
        after = lax.ppermute(first, axis, down)
        x = jnp.concatenate([before, x, after], axis=dim)
    return x


def partner(block, axis, apart):
    count = lax.axis_size(axis)
    route = []
    for low in range(count):
        high = low | 1 << apart
        if high != low and high < count:
            route += [(low, high), (high, low)]
    return lax.ppermute(block, axis, route)


def neighbours(padded):
    return (
        padded[2:, 1:-1, 1:-1],
        padded[:-2, 1:-1, 1:-1],
        padded[1:-1, 2:, 1:-1],
        padded[1:-1, :-2, 1:-1],
        padded[1:-1, 1:-1, 2:],
        padded[1:-1, 1:-1, :-2],
    )


def face_set(padded_k, scale):
    centre = padded_k[1:-1, 1:-1, 1:-1]
    faces = tuple((0.5 * scale * (centre + other) for other in neighbours(padded_k)))
    total = faces[0] + faces[1] + faces[2] + faces[3] + faces[4] + faces[5]
    return (faces, total)


def apply_operator(padded_field, faces, total):
    result = total * padded_field[1:-1, 1:-1, 1:-1]
    for weight, other in zip(faces, neighbours(padded_field)):
        result = result - weight * other
    return result


def restrict(field):
    sx, sy, sz = field.shape
    return field.reshape(sx // 2, 2, sy // 2, 2, sz // 2, 2).mean(axis=(1, 3, 5))


def prolong(field):
    return jnp.repeat(jnp.repeat(jnp.repeat(field, 2, 0), 2, 1), 2, 2)


def field_pad(field):
    rimmed = extended(field, (("gx", 0), ("gy", 1)), 1)
    return jnp.pad(rimmed, ((0, 0), (0, 0), (1, 1)))


def conduct_pad(cond):
    rimmed = extended(cond, (("gx", 0), ("gy", 1)), 1)
    return jnp.pad(rimmed, ((0, 0), (0, 0), (1, 1)))


def merge_blocks(block):
    for bit in range(lax.axis_size("gx").bit_length() - 1):
        other = partner(block, "gx", bit)
        upper = lax.axis_index("gx") >> bit & 1 == 1
        block = jnp.where(
            upper, jnp.concatenate([other, block], 0), jnp.concatenate([block, other], 0)
        )
    for bit in range(lax.axis_size("gy").bit_length() - 1):
        other = partner(block, "gy", bit)
        upper = lax.axis_index("gy") >> bit & 1 == 1
        block = jnp.where(
            upper, jnp.concatenate([other, block], 1), jnp.concatenate([block, other], 1)
        )
    return block


def coarse_solve(coarse_right, coarse_level):
    cfaces, ctotal = coarse_level
    whole = merge_blocks(coarse_right)
    correction = OMEGA * whole / ctotal
    for sweep in range(COARSE_SWEEPS - 1):
        correction = (
            correction
            + OMEGA * (whole - apply_operator(jnp.pad(correction, 1), cfaces, ctotal)) / ctotal
        )
    bx, by, bz = coarse_right.shape
    start_x = lax.axis_index("gx") * bx
    start_y = lax.axis_index("gy") * by
    return lax.dynamic_slice(correction, (start_x, start_y, jnp.int32(0)), (bx, by, bz))


def cycle(levels, coarse_level, level, field, right, first):
    faces, total = levels[level]
    if first:
        field = OMEGA * right / total
    else:
        field = field + OMEGA * (right - apply_operator(field_pad(field), faces, total)) / total
    resid = right - apply_operator(field_pad(field), faces, total)
    coarse_right = restrict(resid)
    if level == 2:
        correction = coarse_solve(coarse_right, coarse_level)
    else:
        correction = cycle(levels, coarse_level, level + 1, None, coarse_right, True)
    field = field + prolong(correction)
    field = field + OMEGA * (right - apply_operator(field_pad(field), faces, total)) / total
    return field


def local(right_side, material, conductivity):
    cond = jnp.zeros(material.shape, jnp.float32)
    for which in range(conductivity.shape[0]):
        cond = jnp.where(material == which, conductivity[which], cond)
    conds = [cond]
    for level in range(3):
        conds.append(restrict(conds[-1]))
    levels = [face_set(conduct_pad(conds[level]), 0.25**level) for level in range(3)]
    coarse_cond = merge_blocks(restrict(conds[2]))
    coarse_level = face_set(jnp.pad(coarse_cond, 1), 0.25**3)
    field = jnp.zeros_like(right_side)
    for turn in range(CYCLES):
        field = cycle(levels, coarse_level, 0, field, right_side, turn == 0)
    return field


def solution(mesh):
    return jax.shard_map(
        local,
        mesh=mesh,
        in_specs=(P("gx", "gy", None), P("gx", "gy", None), P()),
        out_specs=P("gx", "gy", None),
        check_vma=False,
    )
```

profile of v0, /device:TPU:1, one launch (start us, length us, event | category | flops | bytes accessed | tf_op | source)
XLA Modules:
  0.0 521.6 jit_solution(14716648402681302401)
XLA Ops:
  2.0 11.1 %select_select_fusion = f32[16,16,128]{2,1,0:T(8,128)S(1)} fusion(s32[16,16,128]{2,1,0:T(8,128)} %param.4, f32[]{:T(128)} %bitcast.15, f32[]{:T(128)} %bitcast.14, f32[]{:T(128)} %bitcast.13, f32[]{:T(128)} %bitcast.12, f32[]{:T(128)} %bitcast.11, f32[]{:T(128)} %bitcast.10, f32[]{:T(128)} %bitcast.9, f32[]{:T(128)} %bitcast.8, f32[]{:T(128)} %bitcast.7, ...), kind=kLoop, calls=%fused_computation.396 | loop fusion | flops 1048576 | bytes 262208 | tf_op jit(solution)/shard_map/jit(_where)/select_n | solution.py:131
  17.7 5.6 %collective-permute-start = (f32[1,16,128]{2,1,0:T(8,128)S(1)}, f32[1,16,128]{2,1,0:T(8,128)S(1)}, u32[]{:S(2)}, u32[]{:S(2)}) collective-permute-start(f32[1,16,128]{2,1,0:T(8,128)S(1)} %get-tuple-element.59), channel_id=1, source_target_pairs={{16,0},{32,16},{48,32},{64,48},{80,64},{96,80},{112,96},{128,112},... | collective-permute-start | bytes 24584 | tf_op jit(solution)/shard_map/ppermute | solution.py:21
  23.3 9.8 %reshape.84 = f32[8,2,8,2,64,2]{5,4,3,2,1,0:T(8,128)} reshape(f32[16,16,128]{2,1,0:T(8,128)S(1)} %select_select_fusion) | data formatting | bytes 262144 | tf_op jit(solution)/shard_map/reshape | solution.py:63
  65.4 5.3 %collective-permute-start.7 = (f32[18,1,128]{2,1,0:T(1,128)S(1)}, f32[18,1,128]{2,1,0:T(1,128)S(1)}, u32[]{:S(2)}, u32[]{:S(2)}) collective-permute-start(f32[18,1,128]{2,1,0:T(1,128)S(1)} %get-tuple-element.44), channel_id=1, source_target_pairs={{0,1},{1,2},{2,3},{3,4},{4,5},{5,6},{6,7},{7,8},{8,9},{9,10},{10,1... | collective-permute-start | bytes 27656 | tf_op jit(solution)/shard_map/ppermute | solution.py:20
  77.1 9.8 %reshape.83 = f32[8,2,8,2,64,2]{5,4,3,2,1,0:T(8,128)} reshape(f32[16,16,128]{2,1,0:T(8,128)S(1)} %fusion.213) | data formatting | bytes 262144 | tf_op jit(solution)/shard_map/reshape | solution.py:63
  114.5 5.1 collective-permute-start.21
  136.2 13.5 %collective-permute-start.35 = (f32[8,2,16]{2,0,1:T(8,128)S(1)}, f32[8,2,16]{2,0,1:T(8,128)S(1)}, u32[]{:S(2)}, u32[]{:S(2)}) collective-permute-start(f32[8,2,16]{2,0,1:T(8,128)S(1)} %maximum_select_fusion.22), channel_id=1, source_target_pairs={{0,64},{64,0},{16,80},{80,16},{32,96},{96,32},{48,112},{112,48},{1... | collective-permute-start | bytes 3080 | tf_op jit(solution)/shard_map/ppermute | solution.py:33
  178.8 5.8 %collective-permute-start.39 = (f32[64,4,16]{0,2,1:T(8,128)S(1)}, f32[64,4,16]{0,2,1:T(8,128)S(1)}, u32[]{:S(2)}, u32[]{:S(2)}) collective-permute-start(f32[64,4,16]{0,2,1:T(8,128)S(1)} %maximum_select_fusion.12), channel_id=1, source_target_pairs={{0,2},{2,0},{1,3},{3,1},{4,6},{6,4},{5,7},{7,5},{8,10},{10,8},{9,1... | collective-permute-start | bytes 49160 | tf_op jit(solution)/shard_map/ppermute | solution.py:33
  186.6 7.3 %collective-permute-start.40 = (f32[64,8,16]{0,2,1:T(8,128)S(1)}, f32[64,8,16]{0,2,1:T(8,128)S(1)}, u32[]{:S(2)}, u32[]{:S(2)}) collective-permute-start(f32[64,8,16]{0,2,1:T(8,128)S(1)} %maximum_select_fusion.7), channel_id=1, source_target_pairs={{0,4},{4,0},{1,5},{5,1},{2,6},{6,2},{3,7},{7,3},{8,12},{12,8},{9,1... | collective-permute-start | bytes 98312 | tf_op jit(solution)/shard_map/ppermute | solution.py:33
  198.7 9.5 %collective-permute-start.41 = (f32[64,16,16]{0,2,1:T(8,128)S(1)}, f32[64,16,16]{0,2,1:T(8,128)S(1)}, u32[]{:S(2)}, u32[]{:S(2)}) collective-permute-start(f32[64,16,16]{0,2,1:T(8,128)S(1)} %maximum_select_fusion.4), channel_id=1, source_target_pairs={{0,8},{8,0},{1,9},{9,1},{2,10},{10,2},{3,11},{11,3},{4,12},{12,4},... | collective-permute-start | bytes 196616 | tf_op jit(solution)/shard_map/ppermute | solution.py:33
  208.3 6.9 %collective-permute-start.32 = (f32[64,16,16]{0,2,1:T(8,128)S(1)}, f32[64,16,16]{0,2,1:T(8,128)S(1)}, u32[]{:S(2)}, u32[]{:S(2)}) collective-permute-start(f32[64,16,16]{0,2,1:T(8,128)S(1)} %maximum_select_fusion.3), channel_id=1, source_target_pairs={{0,8},{8,0},{1,9},{9,1},{2,10},{10,2},{3,11},{11,3},{4,12},{12,4},... | collective-permute-start | bytes 196616 | tf_op jit(solution)/shard_map/ppermute | solution.py:33
  215.6 12.7 %collective-permute-done.32 = f32[64,16,16]{0,2,1:T(8,128)S(1)} collective-permute-done((f32[64,16,16]{0,2,1:T(8,128)S(1)}, f32[64,16,16]{0,2,1:T(8,128)S(1)}, u32[]{:S(2)}, u32[]{:S(2)}) %collective-permute-start.32) | collective-permute-done | bytes 65568 | tf_op jit(solution)/shard_map/ppermute | solution.py:33
  231.9 10.0 %collective-permute-start.43 = (f32[1,4,32]{2,1,0:T(4,128)S(1)}, f32[1,4,32]{2,1,0:T(4,128)S(1)}, u32[]{:S(2)}, u32[]{:S(2)}) collective-permute-start(f32[1,4,32]{2,1,0:T(4,128)S(1)} %get-tuple-element.94), channel_id=1, source_target_pairs={{0,16},{16,32},{32,48},{48,64},{64,80},{80,96},{96,112},{112,128},... | collective-permute-start | bytes 1544 | tf_op jit(solution)/shard_map/ppermute | solution.py:20
  249.4 5.5 %collective-permute-done.44 = f32[6,1,32]{2,1,0:T(1,128)S(1)} collective-permute-done((f32[6,1,32]{2,1,0:T(1,128)S(1)}, f32[6,1,32]{2,1,0:T(1,128)S(1)}, u32[]{:S(2)}, u32[]{:S(2)}) %collective-permute-start.44) | collective-permute-done | bytes 800 | tf_op jit(solution)/shard_map/ppermute | solution.py:21
  327.1 9.8 %reshape.96 = f32[8,2,8,2,64,2]{5,4,3,2,1,0:T(8,128)} reshape(f32[16,16,128]{2,1,0:T(8,128)S(1)} %fusion.174) | data formatting | bytes 262144 | tf_op jit(solution)/shard_map/reshape | solution.py:63
  362.7 5.2 %collective-permute-start.67 = (f32[1,4,32]{2,1,0:T(4,128)S(1)}, f32[1,4,32]{2,1,0:T(4,128)S(1)}, u32[]{:S(2)}, u32[]{:S(2)}) collective-permute-start(f32[1,4,32]{2,1,0:T(4,128)S(1)} %get-tuple-element.92), channel_id=1, source_target_pairs={{0,16},{16,32},{32,48},{48,64},{64,80},{80,96},{96,112},{112,128},... | collective-permute-start | bytes 1544 | tf_op jit(solution)/shard_map/ppermute | solution.py:20
  385.3 6.6 %collective-permute-start.71 = (f32[4,2,16]{2,0,1:T(4,128)S(1)}, f32[4,2,16]{2,0,1:T(4,128)S(1)}, u32[]{:S(2)}, u32[]{:S(2)}) collective-permute-start(f32[4,2,16]{2,0,1:T(4,128)S(1)} %maximum_select_fusion.26), channel_id=1, source_target_pairs={{0,32},{32,0},{16,48},{48,16},{64,96},{96,64},{80,112},{112,80},{1... | collective-permute-start | bytes 1544 | tf_op jit(solution)/shard_map/ppermute | solution.py:33
  392.9 12.1 %collective-permute-start.72 = (f32[8,2,16]{2,0,1:T(8,128)S(1)}, f32[8,2,16]{2,0,1:T(8,128)S(1)}, u32[]{:S(2)}, u32[]{:S(2)}) collective-permute-start(f32[8,2,16]{2,0,1:T(8,128)S(1)} %maximum_select_fusion.23), channel_id=1, source_target_pairs={{0,64},{64,0},{16,80},{80,16},{32,96},{96,32},{48,112},{112,48},{1... | collective-permute-start | bytes 3080 | tf_op jit(solution)/shard_map/ppermute | solution.py:33
  412.0 9.6 %collective-permute-start.74 = (f32[32,2,16]{2,0,1:T(8,128)S(1)}, f32[32,2,16]{2,0,1:T(8,128)S(1)}, u32[]{:S(2)}, u32[]{:S(2)}) collective-permute-start(f32[32,2,16]{2,0,1:T(8,128)S(1)} %maximum_select_fusion.13), channel_id=1, source_target_pairs={{0,256},{256,0},{16,272},{272,16},{32,288},{288,32},{48,304},{304,... | collective-permute-start | bytes 12296 | tf_op jit(solution)/shard_map/ppermute | solution.py:33
  436.9 5.3 %collective-permute-done.77 = f32[64,8,16]{0,2,1:T(8,128)S(1)} collective-permute-done((f32[64,8,16]{0,2,1:T(8,128)S(1)}, f32[64,8,16]{0,2,1:T(8,128)S(1)}, u32[]{:S(2)}, u32[]{:S(2)}) %collective-permute-start.77) | collective-permute-done | bytes 32800 | tf_op jit(solution)/shard_map/ppermute | solution.py:33
  442.2 7.3 %collective-permute-start.78 = (f32[64,16,16]{0,2,1:T(8,128)S(1)}, f32[64,16,16]{0,2,1:T(8,128)S(1)}, u32[]{:S(2)}, u32[]{:S(2)}) collective-permute-start(f32[64,16,16]{0,2,1:T(8,128)S(1)} %maximum_select_fusion.5), channel_id=1, source_target_pairs={{0,8},{8,0},{1,9},{9,1},{2,10},{10,2},{3,11},{11,3},{4,12},{12,4},... | collective-permute-start | bytes 196616 | tf_op jit(solution)/shard_map/ppermute | solution.py:33
  449.5 10.0 %collective-permute-done.78 = f32[64,16,16]{0,2,1:T(8,128)S(1)} collective-permute-done((f32[64,16,16]{0,2,1:T(8,128)S(1)}, f32[64,16,16]{0,2,1:T(8,128)S(1)}, u32[]{:S(2)}, u32[]{:S(2)}) %collective-permute-start.78) | collective-permute-done | bytes 65568 | tf_op jit(solution)/shard_map/ppermute | solution.py:33
  461.6 10.8 %collective-permute-start.80 = (f32[1,4,32]{2,1,0:T(4,128)S(1)}, f32[1,4,32]{2,1,0:T(4,128)S(1)}, u32[]{:S(2)}, u32[]{:S(2)}) collective-permute-start(f32[1,4,32]{2,1,0:T(4,128)S(1)} %get-tuple-element.90), channel_id=1, source_target_pairs={{0,16},{16,32},{32,48},{48,64},{64,80},{80,96},{96,112},{112,128},... | collective-permute-start | bytes 1544 | tf_op jit(solution)/shard_map/ppermute | solution.py:20
  479.9 5.7 %collective-permute-done.81 = f32[6,1,32]{2,1,0:T(1,128)S(1)} collective-permute-done((f32[6,1,32]{2,1,0:T(1,128)S(1)}, f32[6,1,32]{2,1,0:T(1,128)S(1)}, u32[]{:S(2)}, u32[]{:S(2)}) %collective-permute-start.81) | collective-permute-done | bytes 800 | tf_op jit(solution)/shard_map/ppermute | solution.py:21
  (424 shorter events, 318.7 us)
Async XLA Ops:
  13.1 31.8 %collective-permute-start.1 = (f32[1,16,128]{2,1,0:T(8,128)S(1)}, f32[1,16,128]{2,1,0:T(8,128)S(1)}, u32[]{:S(2)}, u32[]{:S(2)}) collective-permute-start(f32[1,16,128]{2,1,0:T(8,128)S(1)} %get-tuple-element.58), channel_id=1, source_target_pairs={{0,16},{16,32},{32,48},{48,64},{64,80},{80,96},{96,112},{112,128},... | collective-permute-start | bytes 24584 | tf_op jit(solution)/shard_map/ppermute | solution.py:20
  17.7 27.2 %collective-permute-start = (f32[1,16,128]{2,1,0:T(8,128)S(1)}, f32[1,16,128]{2,1,0:T(8,128)S(1)}, u32[]{:S(2)}, u32[]{:S(2)}) collective-permute-start(f32[1,16,128]{2,1,0:T(8,128)S(1)} %get-tuple-element.59), channel_id=1, source_target_pairs={{16,0},{32,16},{48,32},{64,48},{80,64},{96,80},{112,96},{128,112},... | collective-permute-start | bytes 24584 | tf_op jit(solution)/shard_map/ppermute | solution.py:21
  37.1 19.0 %collective-permute-start.9 = (f32[1,8,64]{2,1,0:T(8,128)S(1)}, f32[1,8,64]{2,1,0:T(8,128)S(1)}, u32[]{:S(2)}, u32[]{:S(2)}) collective-permute-start(f32[1,8,64]{2,1,0:T(8,128)S(1)} %get-tuple-element.78), channel_id=1, source_target_pairs={{0,16},{16,32},{32,48},{48,64},{64,80},{80,96},{96,112},{112,128},... | collective-permute-start | bytes 6152 | tf_op jit(solution)/shard_map/ppermute | solution.py:20
  39.0 19.0 %collective-permute-start.8 = (f32[1,8,64]{2,1,0:T(8,128)S(1)}, f32[1,8,64]{2,1,0:T(8,128)S(1)}, u32[]{:S(2)}, u32[]{:S(2)}) collective-permute-start(f32[1,8,64]{2,1,0:T(8,128)S(1)} %get-tuple-element.79), channel_id=1, source_target_pairs={{16,0},{32,16},{48,32},{64,48},{80,64},{96,80},{112,96},{128,112},... | collective-permute-start | bytes 6152 | tf_op jit(solution)/shard_map/ppermute | solution.py:21
  42.9 78.6 %collective-permute-start.33 = (f32[2,2,16]{2,1,0:T(2,128)S(1)}, f32[2,2,16]{2,1,0:T(2,128)S(1)}, u32[]{:S(2)}, u32[]{:S(2)}) collective-permute-start(f32[2,2,16]{2,1,0:T(2,128)S(1)} %broadcast_multiply_fusion.3), channel_id=1, source_target_pairs={{0,16},{16,0},{32,48},{48,32},{64,80},{80,64},{96,112},{112,96},{1... | collective-permute-start | bytes 776 | tf_op jit(solution)/shard_map/ppermute | solution.py:33
  47.6 50.0 %collective-permute-start.16 = (f32[1,4,32]{2,1,0:T(4,128)S(1)}, f32[1,4,32]{2,1,0:T(4,128)S(1)}, u32[]{:S(2)}, u32[]{:S(2)}) collective-permute-start(f32[1,4,32]{2,1,0:T(4,128)S(1)} %get-tuple-element.98), channel_id=1, source_target_pairs={{16,0},{32,16},{48,32},{64,48},{80,64},{96,80},{112,96},{128,112},... | collective-permute-start | bytes 1544 | tf_op jit(solution)/shard_map/ppermute | solution.py:21
  50.8 46.9 %collective-permute-start.17 = (f32[1,4,32]{2,1,0:T(4,128)S(1)}, f32[1,4,32]{2,1,0:T(4,128)S(1)}, u32[]{:S(2)}, u32[]{:S(2)}) collective-permute-start(f32[1,4,32]{2,1,0:T(4,128)S(1)} %get-tuple-element.99), channel_id=1, source_target_pairs={{0,16},{16,32},{32,48},{48,64},{64,80},{80,96},{96,112},{112,128},... | collective-permute-start | bytes 1544 | tf_op jit(solution)/shard_map/ppermute | solution.py:20
  91.1 11.5 %collective-permute-start.13 = (f32[1,8,64]{2,1,0:T(8,128)S(1)}, f32[1,8,64]{2,1,0:T(8,128)S(1)}, u32[]{:S(2)}, u32[]{:S(2)}) collective-permute-start(f32[1,8,64]{2,1,0:T(8,128)S(1)} %get-tuple-element.76), channel_id=1, source_target_pairs={{0,16},{16,32},{32,48},{48,64},{64,80},{80,96},{96,112},{112,128},... | collective-permute-start | bytes 6152 | tf_op jit(solution)/shard_map/ppermute | solution.py:20
  97.7 10.6 %collective-permute-start.19 = (f32[6,1,32]{2,1,0:T(1,128)S(1)}, f32[6,1,32]{2,1,0:T(1,128)S(1)}, u32[]{:S(2)}, u32[]{:S(2)}) collective-permute-start(f32[6,1,32]{2,1,0:T(1,128)S(1)} %get-tuple-element.88), channel_id=1, source_target_pairs={{0,1},{1,2},{2,3},{3,4},{4,5},{5,6},{6,7},{7,8},{8,9},{9,10},{10,1... | collective-permute-start | bytes 2312 | tf_op jit(solution)/shard_map/ppermute | solution.py:20
  124.5 9.3 %collective-permute-start.23 = (f32[6,1,32]{2,1,0:T(1,128)S(1)}, f32[6,1,32]{2,1,0:T(1,128)S(1)}, u32[]{:S(2)}, u32[]{:S(2)}) collective-permute-start(f32[6,1,32]{2,1,0:T(1,128)S(1)} %get-tuple-element.86), channel_id=1, source_target_pairs={{0,1},{1,2},{2,3},{3,4},{4,5},{5,6},{6,7},{7,8},{8,9},{9,10},{10,1... | collective-permute-start | bytes 2312 | tf_op jit(solution)/shard_map/ppermute | solution.py:20
  134.2 15.5 %collective-permute-start.24 = (f32[2,2,16]{2,1,0:T(2,128)S(1)}, f32[2,2,16]{2,1,0:T(2,128)S(1)}, u32[]{:S(2)}, u32[]{:S(2)}) collective-permute-start(f32[2,2,16]{2,1,0:T(2,128)S(1)} %broadcast_multiply_fusion.4), channel_id=1, source_target_pairs={{0,16},{16,0},{32,48},{48,32},{64,80},{80,64},{96,112},{112,96},{1... | collective-permute-start | bytes 776 | tf_op jit(solution)/shard_map/ppermute | solution.py:33
  136.2 17.0 %collective-permute-start.35 = (f32[8,2,16]{2,0,1:T(8,128)S(1)}, f32[8,2,16]{2,0,1:T(8,128)S(1)}, u32[]{:S(2)}, u32[]{:S(2)}) collective-permute-start(f32[8,2,16]{2,0,1:T(8,128)S(1)} %maximum_select_fusion.22), channel_id=1, source_target_pairs={{0,64},{64,0},{16,80},{80,16},{32,96},{96,32},{48,112},{112,48},{1... | collective-permute-start | bytes 3080 | tf_op jit(solution)/shard_map/ppermute | solution.py:33
  175.5 9.1 %collective-permute-start.29 = (f32[64,2,16]{0,2,1:T(8,128)S(1)}, f32[64,2,16]{0,2,1:T(8,128)S(1)}, u32[]{:S(2)}, u32[]{:S(2)}) collective-permute-start(f32[64,2,16]{0,2,1:T(8,128)S(1)} %maximum_select_fusion.16), channel_id=1, source_target_pairs={{0,1},{1,0},{2,3},{3,2},{4,5},{5,4},{6,7},{7,6},{8,9},{9,8},{10,11... | collective-permute-start | bytes 24584 | tf_op jit(solution)/shard_map/ppermute | solution.py:33
  184.6 9.2 %collective-permute-start.30 = (f32[64,4,16]{0,2,1:T(8,128)S(1)}, f32[64,4,16]{0,2,1:T(8,128)S(1)}, u32[]{:S(2)}, u32[]{:S(2)}) collective-permute-start(f32[64,4,16]{0,2,1:T(8,128)S(1)} %maximum_select_fusion.10), channel_id=1, source_target_pairs={{0,2},{2,0},{1,3},{3,1},{4,6},{6,4},{5,7},{7,5},{8,10},{10,8},{9,1... | collective-permute-start | bytes 49160 | tf_op jit(solution)/shard_map/ppermute | solution.py:33
  186.6 12.1 %collective-permute-start.40 = (f32[64,8,16]{0,2,1:T(8,128)S(1)}, f32[64,8,16]{0,2,1:T(8,128)S(1)}, u32[]{:S(2)}, u32[]{:S(2)}) collective-permute-start(f32[64,8,16]{0,2,1:T(8,128)S(1)} %maximum_select_fusion.7), channel_id=1, source_target_pairs={{0,4},{4,0},{1,5},{5,1},{2,6},{6,2},{3,7},{7,3},{8,12},{12,8},{9,1... | collective-permute-start | bytes 98312 | tf_op jit(solution)/shard_map/ppermute | solution.py:33
  193.9 14.3 %collective-permute-start.31 = (f32[64,8,16]{0,2,1:T(8,128)S(1)}, f32[64,8,16]{0,2,1:T(8,128)S(1)}, u32[]{:S(2)}, u32[]{:S(2)}) collective-permute-start(f32[64,8,16]{0,2,1:T(8,128)S(1)} %maximum_select_fusion.6), channel_id=1, source_target_pairs={{0,4},{4,0},{1,5},{5,1},{2,6},{6,2},{3,7},{7,3},{8,12},{12,8},{9,1... | collective-permute-start | bytes 98312 | tf_op jit(solution)/shard_map/ppermute | solution.py:33
  198.7 16.8 %collective-permute-start.41 = (f32[64,16,16]{0,2,1:T(8,128)S(1)}, f32[64,16,16]{0,2,1:T(8,128)S(1)}, u32[]{:S(2)}, u32[]{:S(2)}) collective-permute-start(f32[64,16,16]{0,2,1:T(8,128)S(1)} %maximum_select_fusion.4), channel_id=1, source_target_pairs={{0,8},{8,0},{1,9},{9,1},{2,10},{10,2},{3,11},{11,3},{4,12},{12,4},... | collective-permute-start | bytes 196616 | tf_op jit(solution)/shard_map/ppermute | solution.py:33
  208.3 20.0 %collective-permute-start.32 = (f32[64,16,16]{0,2,1:T(8,128)S(1)}, f32[64,16,16]{0,2,1:T(8,128)S(1)}, u32[]{:S(2)}, u32[]{:S(2)}) collective-permute-start(f32[64,16,16]{0,2,1:T(8,128)S(1)} %maximum_select_fusion.3), channel_id=1, source_target_pairs={{0,8},{8,0},{1,9},{9,1},{2,10},{10,2},{3,11},{11,3},{4,12},{12,4},... | collective-permute-start | bytes 196616 | tf_op jit(solution)/shard_map/ppermute | solution.py:33
  231.9 11.9 %collective-permute-start.43 = (f32[1,4,32]{2,1,0:T(4,128)S(1)}, f32[1,4,32]{2,1,0:T(4,128)S(1)}, u32[]{:S(2)}, u32[]{:S(2)}) collective-permute-start(f32[1,4,32]{2,1,0:T(4,128)S(1)} %get-tuple-element.94), channel_id=1, source_target_pairs={{0,16},{16,32},{32,48},{48,64},{64,80},{80,96},{96,112},{112,128},... | collective-permute-start | bytes 1544 | tf_op jit(solution)/shard_map/ppermute | solution.py:20
  392.9 13.1 %collective-permute-start.72 = (f32[8,2,16]{2,0,1:T(8,128)S(1)}, f32[8,2,16]{2,0,1:T(8,128)S(1)}, u32[]{:S(2)}, u32[]{:S(2)}) collective-permute-start(f32[8,2,16]{2,0,1:T(8,128)S(1)} %maximum_select_fusion.23), channel_id=1, source_target_pairs={{0,64},{64,0},{16,80},{80,16},{32,96},{96,32},{48,112},{112,48},{1... | collective-permute-start | bytes 3080 | tf_op jit(solution)/shard_map/ppermute | solution.py:33
  412.0 11.0 %collective-permute-start.74 = (f32[32,2,16]{2,0,1:T(8,128)S(1)}, f32[32,2,16]{2,0,1:T(8,128)S(1)}, u32[]{:S(2)}, u32[]{:S(2)}) collective-permute-start(f32[32,2,16]{2,0,1:T(8,128)S(1)} %maximum_select_fusion.13), channel_id=1, source_target_pairs={{0,256},{256,0},{16,272},{272,16},{32,288},{288,32},{48,304},{304,... | collective-permute-start | bytes 12296 | tf_op jit(solution)/shard_map/ppermute | solution.py:33
  433.3 8.9 %collective-permute-start.77 = (f32[64,8,16]{0,2,1:T(8,128)S(1)}, f32[64,8,16]{0,2,1:T(8,128)S(1)}, u32[]{:S(2)}, u32[]{:S(2)}) collective-permute-start(f32[64,8,16]{0,2,1:T(8,128)S(1)} %maximum_select_fusion.8), channel_id=1, source_target_pairs={{0,4},{4,0},{1,5},{5,1},{2,6},{6,2},{3,7},{7,3},{8,12},{12,8},{9,1... | collective-permute-start | bytes 98312 | tf_op jit(solution)/shard_map/ppermute | solution.py:33
  442.2 17.3 %collective-permute-start.78 = (f32[64,16,16]{0,2,1:T(8,128)S(1)}, f32[64,16,16]{0,2,1:T(8,128)S(1)}, u32[]{:S(2)}, u32[]{:S(2)}) collective-permute-start(f32[64,16,16]{0,2,1:T(8,128)S(1)} %maximum_select_fusion.5), channel_id=1, source_target_pairs={{0,8},{8,0},{1,9},{9,1},{2,10},{10,2},{3,11},{11,3},{4,12},{12,4},... | collective-permute-start | bytes 196616 | tf_op jit(solution)/shard_map/ppermute | solution.py:33
  461.6 12.7 %collective-permute-start.80 = (f32[1,4,32]{2,1,0:T(4,128)S(1)}, f32[1,4,32]{2,1,0:T(4,128)S(1)}, u32[]{:S(2)}, u32[]{:S(2)}) collective-permute-start(f32[1,4,32]{2,1,0:T(4,128)S(1)} %get-tuple-element.90), channel_id=1, source_target_pairs={{0,16},{16,32},{32,48},{48,64},{64,80},{80,96},{96,112},{112,128},... | collective-permute-start | bytes 1544 | tf_op jit(solution)/shard_map/ppermute | solution.py:20
  (108 other events, 3944.8 us)
where the time goes:
time: 532 us; the launch traced here: 522 us
  starting transfers between devices  314 us (59%)
  waiting for transfers between devices  119 us (22%)
  other arithmetic  43.6 us (8%)
  local copies, waits for them, and re-layouts  42.3 us (8%)
    ppermute x27, starting transfers between devices, partner(): return lax.ppermute(block, axis, route)  136 us
    ppermute x32, starting transfers between devices, extended(): before = lax.ppermute(last, axis, up)  121 us
    ppermute x32, waiting for transfers between devices, extended(): after = lax.ppermute(first, axis, down)  78.8 us
    ppermute x32, starting transfers between devices, extended(): after = lax.ppermute(first, axis, down)  56.8 us
    ppermute x27, waiting for transfers between devices, partner(): return lax.ppermute(block, axis, route)  40.2 us
    reshape x7, local copies, waits for them, and re-layouts, restrict(): field.reshape(sx // 2, 2, sy // 2, 2, sz // 2, 2).mean(axis=(1, 3, 5))  32.4 us
    reduce_sum x9, other arithmetic, restrict(): field.reshape(sx // 2, 2, sy // 2, 2, sz // 2, 2).mean(axis=(1, 3, 5))  13.5 us
    select_n x1, other arithmetic, local(): cond = jnp.where(material == which, conductivity[which], cond)  11.1 us
  transfers between devices with their start and end apart: 91, of which 37 were waited for; matrix products, arithmetic and copies ran while one was open for 6% of the time, Pallas kernels for 0%

commit v1 on v0

v1 whole, which is shorter than its diff:
```python
import functools

import jax
import jax.numpy as jnp
from jax import lax
from jax.experimental import pallas as pl
from jax.experimental.pallas import tpu as pltpu
from jax.sharding import PartitionSpec as P

MESH = pl.DeviceIdType.MESH
CYCLES = 2
SWEEPS = 6
OMEGA = 0.8
NMAT = 16
H = 8
R = 3
DIRS = tuple((a, b) for a in (-1, 0, 1) for b in (-1, 0, 1) if (a, b) != (0, 0))
OPP = tuple(DIRS.index((-a, -b)) for a, b in DIRS)
STEPS = tuple(d for d in range(-R, R + 1) if d)


def send_part(s):
    return {1: slice(8, 16), -1: slice(0, 8), 0: slice(0, 16)}[s]


def halo_part(s):
    return {1: slice(24, 32), -1: slice(0, 8), 0: slice(8, 24)}[s]


def roll(v, shift, axis):
    return pltpu.roll(v, shift % v.shape[axis], axis)


def iota(shape, axis):
    return lax.broadcasted_iota(jnp.int32, shape, axis)


def pair_swap(v, apart, axis):
    low = (iota(v.shape, axis) & apart) == 0
    return jnp.where(low, roll(v, -apart, axis), roll(v, apart, axis))


def kernel(nx, ny, cond, g_hbm, m_hbm, out, *refs):
    names = (
        "G", "M", "K0", "V", "VB", "VE", "I0", "T0", "X0", "YP0", "YM0", "ZP0", "ZM0", "S0", "S1",
        "F0", "K1", "V1", "G1", "VE1", "I1", "X1", "YP1", "YM1", "ZP1", "ZM1", "S2", "F1", "K2",
        "V2", "G2", "VF2", "VE2", "I2", "X2", "YP2", "YM2", "ZP2", "ZM2", "K3", "SX", "SY", "SC",
        "A", "B", "W", "lsem", "gs", "gr", "ms", "mr", "vs", "vr", "ss", "sr", "as_", "ar", "bs",
        "br",
    )
    r = dict(zip(names, refs, strict=True))
    px, py = lax.axis_index("gx"), lax.axis_index("gy")

    def exists(a, b=0):
        x, y = px + a, py + b
        return (x >= 0) & (x < nx) & (y >= 0) & (y < ny)

    def dev(a, b):
        return (px + a, py + b)

    own = (slice(8, 24), slice(8, 24))
    lg = pltpu.make_async_copy(g_hbm, r["G"].at[own], r["lsem"].at[0])
    lm = pltpu.make_async_copy(m_hbm, r["M"].at[own], r["lsem"].at[1])
    lg.start()
    lm.start()
    others = [(a, b) for a, b in DIRS] + [(d, 0) for d in STEPS if abs(d) > 1]
    others += [(0, d) for d in STEPS if abs(d) > 1]
    barrier = pltpu.get_barrier_semaphore()
    zero8 = jnp.zeros((8, 32, 128), jnp.float32)
    for name, fill in (("G", 0.0), ("VB", 0.0), ("M", NMAT)):
        ref = r[name]
        dt = ref.dtype
        for s in (slice(0, 8), slice(24, 32)):
            ref[s] = jnp.full((8, 32, 128), fill, dt)
            ref[8:24, s] = jnp.full((16, 8, 128), fill, dt)
    r["A"][...] = jnp.zeros(r["A"].shape, jnp.float32)
    r["B"][...] = jnp.zeros(r["B"].shape, jnp.float32)
    for n in ("SX", "SY", "SC"):
        r[n][...] = jnp.zeros(r[n].shape, jnp.float32)
    count = jnp.int32(0)
    for a, b in others:
        ok = exists(a, b)
        count = count + jnp.where(ok, 1, 0)

        @pl.when(ok)
        def _(a=a, b=b):
            pl.semaphore_signal(barrier, inc=1, device_id=dev(a, b), device_id_type=MESH)

    pl.semaphore_wait(barrier, count)

    def halo_copy(src, dst, ssem, rsem, i, sending):
        a, b = DIRS[i]
        if sending:
            there = (halo_part(-a), halo_part(-b))
            return pltpu.make_async_remote_copy(
                src_ref=src.at[send_part(a), send_part(b)],
                dst_ref=dst.at[there],
                send_sem=ssem.at[i],
                recv_sem=rsem.at[OPP[i]],
                device_id=dev(a, b),
                device_id_type=MESH,
            )
        here = dst.at[halo_part(a), halo_part(b)]
        return pltpu.make_async_remote_copy(
            src_ref=here, dst_ref=here, send_sem=ssem.at[i], recv_sem=rsem.at[i],
            device_id=dev(a, b), device_id_type=MESH,
        )

    def each(fn, dirs=range(len(DIRS))):
        for i in dirs:
            pl.when(exists(*DIRS[i]))(functools.partial(fn, i))

    def send_halo(src, dst, ssem, rsem):
        each(lambda i: halo_copy(src, dst, ssem, rsem, i, True).start())

    def recv_halo(dst, ssem, rsem):
        each(lambda i: halo_copy(None, dst, ssem, rsem, i, False).wait_recv())

    def sent_halo(src, dst, ssem, rsem):
        each(lambda i: halo_copy(src, dst, ssem, rsem, i, True).wait_send())

    send_halo(m_hbm, r["M"], r["ms"], r["mr"])
    send_halo(g_hbm, r["G"], r["gs"], r["gr"])

    lane = iota((8, 128), 1)
    table = jnp.zeros((8, 128), jnp.float32)
    for i in range(NMAT):
        table = jnp.where(lane == i, cond[i], table)
    lm.wait()
    recv_halo(r["M"], r["ms"], r["mr"])
    table32 = jnp.concatenate([table] * 4, 0)

    def look(i, _):
        r["K0"][i] = jnp.take_along_axis(table32, r["M"][i], axis=1)
        return 0

    lax.fori_loop(0, 32, look, 0)

    def faces(lv, planes, first, last):
        scale = 0.5 * 0.25**lv
        step = 1 << lv
        k_ref = r[f"K{lv}"]
        x_ref = r[f"X{lv}"]
        x_ref[first - 1] = scale * (k_ref[first - 1] + k_ref[first])

        def body(i, _):
            k = k_ref[i]
            ln = iota(k.shape, 1)
            wx = scale * (k + k_ref[i + 1])
            wm = x_ref[i - 1]
            yp = scale * (k + roll(k, -1, 0))
            ym = scale * (k + roll(k, 1, 0))
            zp = scale * (k + jnp.where(ln < 128 - step, roll(k, -step, 1), 0.0))
            zm = scale * (k + jnp.where(ln >= step, roll(k, step, 1), 0.0))
            total = wx + wm + yp + ym + zp + zm
            inside = k > 0.0
            x_ref[i] = wx
            r[f"YP{lv}"][i] = yp
            r[f"YM{lv}"][i] = ym
            r[f"ZP{lv}"][i] = jnp.where(ln < 128 - step, zp, 0.0)
            r[f"ZM{lv}"][i] = jnp.where(ln >= step, zm, 0.0)
            inv = jnp.where(inside, OMEGA / jnp.where(inside, total, 1.0), 0.0)
            r[f"I{lv}"][i] = inv
            if lv == 0:
                r["T0"][i] = total
                r["V"][i] = inv * r["G"][i]
            return 0

        lax.fori_loop(first, last, body, 0)

    def around(lv, v_ref, i):
        step = 1 << lv
        v = v_ref[i]
        x = r[f"X{lv}"]
        n = x[i] * v_ref[i + 1] + x[i - 1] * v_ref[i - 1]
        n = n + r[f"YP{lv}"][i] * roll(v, -1, 0) + r[f"YM{lv}"][i] * roll(v, 1, 0)
        return v, n + r[f"ZP{lv}"][i] * roll(v, -step, 1) + r[f"ZM{lv}"][i] * roll(v, step, 1)

    def z_mean(s, lv):
        return 0.125 * (s + pair_swap(s, 1 << lv, 1))

    def k1_sum(i, _):
        r["S0"][i] = r["K0"][2 * i] + r["K0"][2 * i + 1]
        return 0

    lax.fori_loop(0, 16, k1_sum, 0)

    def k1_mean(i, _):
        s = r["S0"][i, pl.ds(0, 16, 2), :] + r["S0"][i, pl.ds(1, 16, 2), :]
        r["K1"][i] = z_mean(s, 0)
        return 0

    lax.fori_loop(0, 16, k1_mean, 0)

    def k2_sum(i, _):
        r["S1"][i] = r["K1"][2 * i] + r["K1"][2 * i + 1]
        return 0

    lax.fori_loop(0, 8, k2_sum, 0)

    def k2_mean(i, _):
        s = r["S1"][i, pl.ds(0, 8, 2), :] + r["S1"][i, pl.ds(1, 8, 2), :]
        r["K2"][i] = z_mean(s, 1)
        return 0

    lax.fori_loop(0, 8, k2_mean, 0)

    def to_three(t):
        t = t + pair_swap(t, 1, 0)
        return z_mean(t, 2)

    for i in range(4):
        r["K3"][i] = to_three(r["K2"][2 * i] + r["K2"][2 * i + 1])

    scale3 = 0.5 * 0.25**3
    inv3 = []
    for i in (1, 2):
        k = r["K3"][i]
        s = r["K3"][i - 1] + r["K3"][i + 1] + roll(k, 2, 0) + roll(k, -2, 0)
        s = s + jnp.where(lane < 120, roll(k, -8, 1), 0.0) + jnp.where(lane >= 8, roll(k, 8, 1), 0.0)
        t = scale3 * (6.0 * k + s)
        ok = k > 0.0
        inv3.append(jnp.where(ok, OMEGA / jnp.where(ok, t, 1.0), 0.0))

    lg.wait()
    recv_halo(r["G"], r["gs"], r["gr"])
    faces(0, 32, 1, 31)
    faces(1, 16, 1, 15)
    faces(2, 8, 1, 7)

    row = iota((8, 128), 0)
    slot = lane & 7
    coarse_w = None

    def z_copies(d, cyc, sending):
        a = r["A"].at[cyc]
        if sending:
            return pltpu.make_async_remote_copy(
                src_ref=a.at[R], dst_ref=a.at[R - d], send_sem=r["as_"].at[cyc, d + R],
                recv_sem=r["ar"].at[cyc, R - d], device_id=dev(0, d), device_id_type=MESH,
            )
        return pltpu.make_async_remote_copy(
            src_ref=a.at[R + d], dst_ref=a.at[R + d], send_sem=r["as_"].at[cyc, d + R],
            recv_sem=r["ar"].at[cyc, R + d], device_id=dev(0, d), device_id_type=MESH,
        )

    def x_copies(d, cyc, sending):
        b = r["B"].at[cyc]

        def part(s):
            return b.at[pl.ds(8 * s, 8)]

        if sending:
            return pltpu.make_async_remote_copy(
                src_ref=part(R), dst_ref=part(R - d), send_sem=r["bs"].at[cyc, d + R],
                recv_sem=r["br"].at[cyc, R - d], device_id=dev(d, 0), device_id_type=MESH,
            )
        return pltpu.make_async_remote_copy(
            src_ref=part(R + d), dst_ref=part(R + d), send_sem=r["bs"].at[cyc, d + R],
            recv_sem=r["br"].at[cyc, R + d], device_id=dev(d, 0), device_id_type=MESH,
        )

    far_first = sorted(STEPS, key=lambda d: -abs(d))

    def side_buf(a, b, cyc):
        if b == 0:
            return r["SX"].at[cyc, (a + 1) // 2]
        if a == 0:
            return r["SY"].at[cyc, (b + 1) // 2]
        return r["SC"].at[cyc, (a + 1) + (b + 1) // 2]

    def side_src(a):
        return {1: slice(4, 6), -1: slice(2, 4), 0: slice(2, 6)}[a]

    def side_copy(i, cyc, sending):
        a, b = DIRS[i]
        if sending:
            return pltpu.make_async_remote_copy(
                src_ref=r["V2"].at[cyc, side_src(a)], dst_ref=side_buf(-a, -b, cyc),
                send_sem=r["ss"].at[cyc, i], recv_sem=r["sr"].at[cyc, OPP[i]],
                device_id=dev(a, b), device_id_type=MESH,
            )
        here = side_buf(a, b, cyc)
        return pltpu.make_async_remote_copy(
            src_ref=here, dst_ref=here, send_sem=r["ss"].at[cyc, i], recv_sem=r["sr"].at[cyc, i],
            device_id=dev(a, b), device_id_type=MESH,
        )

    for cyc in range(CYCLES):
        if cyc:
            recv_halo(r["VB"], r["vs"], r["vr"])

            def sweep(i, _):
                v, n = around(0, r["VB"], i)
                r["V"][i] = (1.0 - OMEGA) * v + r["I0"][i] * (r["G"][i] + n)
                return 0

            lax.fori_loop(1, 31, sweep, 0)

        def resid0(i, first=cyc == 0):
            v, n = around(0, r["V"], i)
            if first:
                return (1.0 - OMEGA) * r["G"][i] + n
            return r["G"][i] - r["T0"][i] * v + n

        def down0(i, _):
            r["S0"][i] = resid0(2 * i) + resid0(2 * i + 1)
            return 0

        lax.fori_loop(1, 15, down0, 0)

        def start1(i, _):
            s = r["S0"][i, pl.ds(0, 16, 2), :] + r["S0"][i, pl.ds(1, 16, 2), :]
            g = z_mean(s, 0)
            r["G1"][i] = g
            r["V1"][i] = r["I1"][i] * g
            return 0

        lax.fori_loop(1, 15, start1, 0)

        def resid1(i):
            _, n = around(1, r["V1"], i)
            return (1.0 - OMEGA) * r["G1"][i] + n

        def down1(i, _):
            r["S1"][i] = resid1(2 * i) + resid1(2 * i + 1)
            return 0

        lax.fori_loop(1, 7, down1, 0)
        v2 = r["V2"].at[cyc]

        def start2(i, _):
            s = r["S1"][i, pl.ds(0, 8, 2), :] + r["S1"][i, pl.ds(1, 8, 2), :]
            g = z_mean(s, 1)
            r["G2"][i] = g
            v2[i] = r["I2"][i] * g
            return 0

        lax.fori_loop(1, 7, start2, 0)

        def resid2(i):
            _, n = around(2, v2, i)
            return (1.0 - OMEGA) * r["G2"][i] + n

        first3 = []
        for a in (0, 1):
            t = resid2(2 * a + 2) + resid2(2 * a + 3)
            first3.append(inv3[a] * to_three(t))
        tile = jnp.zeros((8, 128), jnp.float32)
        for f, pair in ((0, first3), (1, [r["K3"][1], r["K3"][2]])):
            for a in (0, 1):
                moved = roll(pair[a], 4 * f + a - 2, 0)
                tile = jnp.where((row == 4 * f + a) | (row == 4 * f + a + 2), moved, tile)
        r["A"][cyc, R] = tile
        for d in far_first:
            pl.when(exists(0, d))(lambda d=d, c=cyc: z_copies(d, c, True).start())
        each(lambda i, c=cyc: side_copy(i, c, True).start())
        for d in STEPS:
            pl.when(exists(0, d))(lambda d=d, c=cyc: z_copies(d, c, False).wait_recv())
        packed = jnp.zeros((8, 128), jnp.float32)
        for s in range(2 * R + 1):
            packed = jnp.where(slot == s, r["A"][cyc, s], packed)
        r["B"][cyc, pl.ds(8 * R, 8)] = packed
        for d in far_first:
            pl.when(exists(d, 0))(lambda d=d, c=cyc: x_copies(d, c, True).start())

        each(lambda i, c=cyc: side_copy(i, c, False).wait_recv())
        low, high = row < 2, row >= 6

        def ring(xs, mid, ys_low, ys_high):
            return jnp.where(low, roll(ys_low, -4, 0), jnp.where(high, roll(ys_high, 4, 0), mid))

        for i in range(8):
            if i < 2:
                args = (r["SX"][cyc, 0, i], r["SC"][cyc, 0, i], r["SC"][cyc, 1, i])
            elif i < 6:
                args = (v2[i], r["SY"][cyc, 0, i - 2], r["SY"][cyc, 1, i - 2])
            else:
                args = (r["SX"][cyc, 1, i - 6], r["SC"][cyc, 2, i - 6], r["SC"][cyc, 3, i - 6])
            r["VF2"][i] = ring(None, *args)

        for d in STEPS:
            pl.when(exists(d, 0))(lambda d=d, c=cyc: x_copies(d, c, False).wait_recv())

        def got(f, b, a):
            return r["B"][cyc, pl.ds(4 * f + 2 * b + a, 8, 8), :]

        def sides(c, b, a):
            xp = c[b][1] if a == 0 else roll(c[b][0], -1, 0)
            xm = c[b][0] if a == 1 else roll(c[b][1], 1, 0)
            yp = c[1][a] if b == 0 else roll(c[0][a], -1, 1)
            ym = c[0][a] if b == 1 else roll(c[1][a], 1, 1)
            return xp, xm, yp, ym, roll(c[b][a], -8, 1), roll(c[b][a], 8, 1)

        if cyc == 0:
            k3 = [[got(1, b, a) for a in (0, 1)] for b in (0, 1)]
            coarse_w = {}
            for b in (0, 1):
                for a in (0, 1):
                    k = k3[b][a]
                    ns = list(sides(k3, b, a))
                    ns[4] = jnp.where(lane < 120, ns[4], 0.0)
                    ns[5] = jnp.where(lane >= 8, ns[5], 0.0)
                    ws = [scale3 * (k + n) for n in ns]
                    total = ws[0] + ws[1] + ws[2] + ws[3] + ws[4] + ws[5]
                    ok = k > 0.0
                    inv = jnp.where(ok, OMEGA / jnp.where(ok, total, 1.0), 0.0)
                    ws[4] = jnp.where(lane < 120, ws[4], 0.0)
                    ws[5] = jnp.where(lane >= 8, ws[5], 0.0)
                    base = 7 * (2 * b + a)
                    for j, w in enumerate(ws):
                        r["W"][base + j] = inv * w
        start = [[got(0, b, a) for a in (0, 1)] for b in (0, 1)]

        def coarse(_, flat):
            c = [[flat[0], flat[1]], [flat[2], flat[3]]]
            new = []
            for b in (0, 1):
                for a in (0, 1):
                    base = 7 * (2 * b + a)
                    v = start[b][a] + (1.0 - OMEGA) * c[b][a]
                    for j, n in enumerate(sides(c, b, a)):
                        v = v + r["W"][base + j] * n
                    new.append(v)
            return tuple(new)

        flat = (start[0][0], start[0][1], start[1][0], start[1][1])
        flat = lax.fori_loop(0, SWEEPS - 1, coarse, flat)

        cell = row // 2
        want = (lane & ~7) + (R - 1) + (cell + 1) // 2
        for i in range(4):
            s, a = R - 1 + (i + 1) // 2, (i + 1) % 2
            e0 = jnp.broadcast_to(flat[a][s : s + 1], (8, 128))
            e1 = jnp.broadcast_to(flat[2 + a][s : s + 1], (8, 128))
            e = jnp.take_along_axis(jnp.where(cell % 2 == 0, e1, e0), want, axis=1)
            r["VE2"][2 * i] = r["VF2"][2 * i] + e
            r["VE2"][2 * i + 1] = r["VF2"][2 * i + 1] + e

        def up2(i, _):
            v, n = around(2, r["VE2"], i)
            v = (1.0 - OMEGA) * v + r["VF2"][i] + r["I2"][i] * n
            r["S2"][i, pl.ds(0, 8, 2), :] = v
            r["S2"][i, pl.ds(1, 8, 2), :] = v
            return 0

        lax.fori_loop(1, 7, up2, 0)

        def add1(i, _):
            e = r["S2"][i]
            r["VE1"][2 * i] = r["V1"][2 * i] + e
            r["VE1"][2 * i + 1] = r["V1"][2 * i + 1] + e
            return 0

        lax.fori_loop(1, 7, add1, 0)

        def up1(i, _):
            v, n = around(1, r["VE1"], i)
            v = (1.0 - OMEGA) * v + r["V1"][i] + r["I1"][i] * n
            r["F1"][i, pl.ds(0, 16, 2), :] = v
            r["F1"][i, pl.ds(1, 16, 2), :] = v
            return 0

        lax.fori_loop(3, 13, up1, 0)

        def add0(i, _):
            e = r["F1"][i]
            r["VE"][2 * i] = r["V"][2 * i] + e
            r["VE"][2 * i + 1] = r["V"][2 * i + 1] + e
            return 0

        lax.fori_loop(3, 13, add0, 0)

        def up0(i, _, c=cyc):
            v, n = around(0, r["VE"], i)
            if c == 0:
                v = (1.0 - OMEGA) * v + r["V"][i] + r["I0"][i] * n
            else:
                v = (1.0 - OMEGA) * v + r["I0"][i] * (r["G"][i] + n)
            if c == CYCLES - 1:
                out[i - 8] = v[8:24]
            else:
                r["VB"][i, 8:24] = v[8:24]
                r["F0"][i - 8] = v[8:24]
            return 0

        lax.fori_loop(8, 24, up0, 0)
        if cyc < CYCLES - 1:
            send_halo(r["F0"], r["VB"], r["vs"], r["vr"])

    sent_halo(m_hbm, r["M"], r["ms"], r["mr"])
    sent_halo(g_hbm, r["G"], r["gs"], r["gr"])
    sent_halo(r["F0"], r["VB"], r["vs"], r["vr"])
    for cyc in range(CYCLES):
        each(lambda i, c=cyc: side_copy(i, c, True).wait_send())
        for d in STEPS:
            pl.when(exists(0, d))(lambda d=d, c=cyc: z_copies(d, c, True).wait_send())
            pl.when(exists(d, 0))(lambda d=d, c=cyc: x_copies(d, c, True).wait_send())


def scratch():
    f = jnp.float32

    def vm(*shape):
        return pltpu.VMEM(shape, f)

    a, b, c = vm(32, 32, 128), vm(16, 16, 128), vm(8, 8, 128)
    dma = pltpu.SemaphoreType.DMA
    nd, ns = len(DIRS), 2 * R + 1
    shapes = [a, pltpu.VMEM((32, 32, 128), jnp.int32)] + [a] * 11
    shapes += [vm(16, 32, 128), vm(8, 16, 128), vm(16, 16, 128)]
    shapes += [b] * 10 + [vm(8, 16, 128), vm(16, 32, 128)]
    shapes += [c, vm(CYCLES, 8, 8, 128)] + [c] * 9 + [vm(4, 8, 128)]
    shapes += [vm(CYCLES, 2, 2, 8, 128), vm(CYCLES, 2, 4, 8, 128), vm(CYCLES, 4, 2, 8, 128)]
    shapes += [vm(CYCLES, ns, 8, 128), vm(CYCLES, 64, 128), vm(28, 8, 128)]
    shapes += [dma((2,))] + [dma((nd,))] * 6 + [dma((CYCLES, nd))] * 2 + [dma((CYCLES, ns))] * 4
    return shapes


def local(right_side, material, conductivity):
    nx, ny = lax.axis_size("gx"), lax.axis_size("gy")
    return pl.pallas_call(
        functools.partial(kernel, nx, ny),
        out_shape=jax.ShapeDtypeStruct(right_side.shape, right_side.dtype),
        in_specs=[
            pl.BlockSpec(memory_space=pltpu.SMEM),
            pl.BlockSpec(memory_space=pl.ANY),
            pl.BlockSpec(memory_space=pl.ANY),
        ],
        out_specs=pl.BlockSpec(memory_space=pltpu.VMEM),
        scratch_shapes=scratch(),
        compiler_params=pltpu.CompilerParams(collective_id=0, has_side_effects=True),
        name="vcycles",
    )(conductivity, right_side, material)


def solution(mesh):
    return jax.shard_map(
        local,
        mesh=mesh,
        in_specs=(P("gx", "gy", None), P("gx", "gy", None), P()),
        out_specs=P("gx", "gy", None),
        check_vma=False,
    )
```

time: 532 us -> 68 us (0.13); the launches traced: 522 us -> 66.8 us
  starting transfers between devices: 314 us -> 0 us
  waiting for transfers between devices: 119 us -> 0 us
  Pallas kernels: 0 us -> 65.2 us
  other arithmetic: 43.6 us -> 0 us
  local copies, waits for them, and re-layouts: 42.3 us -> 1.57 us
    ppermute x91 -> x0, starting transfers between devices: 314 us -> none  [the longest x27 136 us: partner(): return lax.ppermute(block, axis, route)]
    ppermute x91 -> x0, waiting for transfers between devices: 119 us -> none  [the longest x32 78.8 us: extended(): after = lax.ppermute(first, axis, down)]
    pallas_call x0 -> x1, Pallas kernels: none -> 65.2 us  [local(): pl.pallas_call(functools.partial(kernel, nx, ny), out_shape=jax.ShapeDtyp...]
    reshape x19 -> x0, local copies, waits for them, and re-layouts: 36.1 us -> none  [the longest x7 32.4 us: restrict(): field.reshape(sx // 2, 2, sy // 2, 2, sz // 2, 2).mean(axis=(1, 3, 5))]
    reduce_sum x9 -> x0, other arithmetic: 13.5 us -> none  [restrict(): field.reshape(sx // 2, 2, sy // 2, 2, sz // 2, 2).mean(axis=(1, 3, 5))]
    select_n x26 -> x0, other arithmetic: 11.5 us -> none  [the longest x1 11.1 us: local(): cond = jnp.where(material == which, conductivity[which], cond)]
    add x23 -> x0, other arithmetic: 11 us -> none  [the longest x7 6.73 us: cycle(): field + OMEGA * (right - apply_operator(field_pad(field), faces, total))...]
  transfers between devices with their start and end apart: 91 -> 0, of which waited for: 37 -> 0; matrix products, arithmetic and copies ran while one was open for 6% -> 0% of each run, Pallas kernels for 0% -> 0%
where the time goes in v1:
time: 68 us; the launch traced here: 66.8 us
  Pallas kernels  65.2 us (96%)
  local copies, waits for them, and re-layouts  1.57 us (2%)
    pallas_call x1, Pallas kernels, local(): pl.pallas_call(functools.partial(kernel, nx, ny), out_shape=jax.ShapeDtyp...  65.2 us
    unnamed x1, local copies, waits for them, and re-layouts  1.57 us

profile of v1, /device:TPU:1, one launch (start us, length us, event | category | flops | bytes accessed | tf_op | source)
XLA Modules:
  0.0 66.8 jit_solution(16803406361067425714)
XLA Ops:
  0.0 65.2 %vcycles.1 = f32[16,16,128]{2,1,0:T(8,128)} custom-call(f32[16]{0:T(128)} %cond.1, f32[16,16,128]{2,1,0:T(8,128)} %g_hbm.1, s32[16,16,128]{2,1,0:T(8,128)} %m_hbm.1), custom_call_target="tpu_custom_call" | custom-call | tf_op jit(solution)/shard_map/vcycles/pallas_call | solution.py:522
  65.2 1.6 %copy.5 = f32[16,16,128]{2,1,0:T(8,128)} copy(f32[16,16,128]{2,1,0:T(8,128)} %vcycles.1) | data formatting | bytes 262144

commit v2 on v0

v2 whole, which is shorter than its diff:
```python
import functools

import jax
import jax.numpy as jnp
from jax import lax
from jax.experimental import pallas as pl
from jax.experimental.pallas import tpu as pltpu
from jax.sharding import PartitionSpec as P

MESH = pl.DeviceIdType.MESH
CYCLES = 2
SWEEPS = 6
OMEGA = 0.8
NMAT = 16
H = 8
R = 3
DIRS = tuple((a, b) for a in (-1, 0, 1) for b in (-1, 0, 1) if (a, b) != (0, 0))


STEPS = tuple(range(-R, R + 1))
PARTNERS = tuple(
    sorted(
        ((a, b) for a in STEPS for b in STEPS if (a or b) and abs(a) + abs(b) <= R + 1),
        key=lambda d: -abs(d[0]) - 1.25 * abs(d[1]),
    )
)
G_CUT, V_CUT = 6, 7


def send_part(s, n=H):
    return {1: slice(16 - n, 16), -1: slice(0, n), 0: slice(0, 16)}[s]


def halo_part(s, n=H):
    return {1: slice(24, 24 + n), -1: slice(8 - n, 8), 0: slice(8, 24)}[s]


def roll(v, shift, axis):
    return pltpu.roll(v, shift % v.shape[axis], axis)


def iota(shape, axis):
    return lax.broadcasted_iota(jnp.int32, shape, axis)


def pair_swap(v, apart, axis):
    low = (iota(v.shape, axis) & apart) == 0
    return jnp.where(low, roll(v, -apart, axis), roll(v, apart, axis))


def kernel(nx, ny, cond, g_hbm, m_hbm, out, *refs):
    names = (
        "G", "M", "K0", "V", "VB", "VE", "I0", "T0", "X0", "Y0", "Z0", "S0", "F1",
        "K1", "V1", "G1", "VE1", "I1", "X1", "Y1", "Z1", "S1", "S2",
        "K2", "V2", "VF2", "VE2", "I2", "X2", "Y2", "Z2", "K3", "F0", "C", "W",
        "lsem", "send", "recv", "ready",
    )
    r = dict(zip(names, refs, strict=True))
    px, py = lax.axis_index("gx"), lax.axis_index("gy")
    xs = {d: lax.rem(px + (d + nx), nx) if d else px for d in STEPS}
    ys = {d: lax.rem(py + (d + ny), ny) if d else py for d in STEPS}

    def dev(a, b):
        return (xs[a], ys[b])

    def remote(src, dst, sem, a, b):
        return pltpu.make_async_remote_copy(
            src_ref=src, dst_ref=dst, send_sem=r["send"].at[sem], recv_sem=r["recv"].at[sem],
            device_id=dev(a, b), device_id_type=MESH,
        )

    own = (slice(8, 24), slice(8, 24))
    lg = pltpu.make_async_copy(g_hbm, r["G"].at[own], r["lsem"].at[0])
    lm = pltpu.make_async_copy(m_hbm, r["M"].at[own], r["lsem"].at[1])
    lm.start()
    lg.start()
    barrier = pltpu.get_barrier_semaphore()
    for a, b in DIRS:
        pl.semaphore_signal(barrier, inc=1, device_id=dev(a, b), device_id_type=MESH)
    lane = iota((8, 128), 1)
    row = iota((8, 128), 0)
    slot = lane & 7
    table = jnp.zeros((8, 128), jnp.float32)
    for i in range(NMAT):
        table = jnp.where(lane == i, cond[i], table)
    table32 = jnp.concatenate([table] * 4, 0)
    pl.semaphore_wait(barrier, len(DIRS))

    def send_halo(src, dst, sem, cut):
        for a, b in DIRS:
            n = cut if a and b else H
            remote(
                src.at[send_part(a, n), send_part(b)],
                dst.at[halo_part(-a, n), halo_part(-b)],
                sem, a, b,
            ).start()

    def all_halos(dst, cut):
        view = dst.at[0 : (512 + 4 * H * cut) // 32]
        sem = {"M": M_SEM, "G": G_SEM, "VB": V_SEM}
        for name in sem:
            if dst is r[name]:
                return remote(view, view, sem[name], 1, 0)
        raise ValueError

    def clear_edges(ref, value):
        full = functools.partial(jnp.full, fill_value=value, dtype=ref.dtype)

        @pl.when(px == 0)
        def _():
            ref[0:8] = full((8, 32, 128))

        @pl.when(px == nx - 1)
        def _():
            ref[24:32] = full((8, 32, 128))

        @pl.when(py == 0)
        def _():
            ref[:, 0:8] = full((32, 8, 128))

        @pl.when(py == ny - 1)
        def _():
            ref[:, 24:32] = full((32, 8, 128))

    send_halo(m_hbm, r["M"], M_SEM, H)
    send_halo(g_hbm, r["G"], G_SEM, G_CUT)
    lm.wait()
    all_halos(r["M"], H).wait_recv()
    for a, b in ((-1, 0), (1, 0), (0, -1), (0, 1)):
        pl.semaphore_signal(r["ready"], inc=1, device_id=dev(a, b), device_id_type=MESH)
    clear_edges(r["M"], NMAT)

    def planes(lo, hi, step, one):
        def body(j, _):
            done = []
            for q in range(step):
                done += one(lo + j * step + q)
            for ref, i, v in done:
                ref[i] = v
            return 0

        lax.fori_loop(0, (hi - lo) // step, body, 0)

    def unrolled(lo, hi, one):
        done = []
        for i in range(lo, hi):
            done += one(i)
        for ref, i, v in done:
            ref[i] = v

    def face_values(lv, i):
        scale = 0.5 * 0.25**lv
        step = 1 << lv
        k_ref = r[f"K{lv}"]
        k, kn = k_ref[i], k_ref[i + 1]
        ln = iota(k.shape, 1)
        below, above = ln < 128 - step, ln >= step
        ky = roll(k, -1, 0)
        kz = roll(k, -step, 1)
        s = 6.0 * k + (kn + k_ref[i - 1]) + (ky + roll(k, 1, 0))
        s = s + jnp.where(below, kz, 0.0) + jnp.where(above, roll(k, step, 1), 0.0)
        total = scale * s
        inside = k > 0.0
        inv = jnp.where(inside, OMEGA / jnp.where(inside, total, 1.0), 0.0)
        res = [
            (r[f"X{lv}"], i, scale * (k + kn)),
            (r[f"Y{lv}"], i, scale * (k + ky)),
            (r[f"Z{lv}"], i, jnp.where(below, scale * (k + kz), 0.0)),
            (r[f"I{lv}"], i, inv),
        ]
        if lv == 0:
            res.append((r["T0"], i, total))
        return res

    def around(lv, v_ref, i):
        step = 1 << lv
        v = v_ref[i]
        x, y, z = r[f"X{lv}"], r[f"Y{lv}"][i], r[f"Z{lv}"][i]
        n = x[i] * v_ref[i + 1] + x[i - 1] * v_ref[i - 1]
        n = n + (y * roll(v, -1, 0) + roll(y * v, 1, 0))
        return v, n + (z * roll(v, -step, 1) + roll(z * v, step, 1))

    def z_mean(s, lv):
        return 0.125 * (s + pair_swap(s, 1 << lv, 1))

    def y_pairs(ref, i, n):
        return ref[i, pl.ds(0, n, 2), :] + ref[i, pl.ds(1, n, 2), :]

    def to_three(t):
        return z_mean(t + pair_swap(t, 1, 0), 2)

    def look(i):
        k = [jnp.take_along_axis(table32, r["M"][2 * i + q], axis=1) for q in (0, 1)]
        return [(r["K0"], 2 * i, k[0]), (r["K0"], 2 * i + 1, k[1]), (r["S0"], i, k[0] + k[1])]

    planes(0, 16, 4, look)
    planes(0, 16, 8, lambda i: [(r["K1"], i, z_mean(y_pairs(r["S0"], i, 16), 0))])
    unrolled(0, 8, lambda i: [(r["S1"], i, r["K1"][2 * i] + r["K1"][2 * i + 1])])
    unrolled(0, 8, lambda i: [(r["K2"], i, z_mean(y_pairs(r["S1"], i, 8), 1))])
    unrolled(0, 4, lambda i: [(r["K3"], i, to_three(r["K2"][2 * i] + r["K2"][2 * i + 1]))])
    for lv, scale in ((0, 0.5), (1, 0.125), (2, 0.03125)):
        r[f"X{lv}"][0] = scale * (r[f"K{lv}"][0] + r[f"K{lv}"][1])
    planes(1, 31, 3, functools.partial(face_values, 0))
    planes(1, 15, 7, functools.partial(face_values, 1))
    unrolled(1, 7, functools.partial(face_values, 2))

    scale3 = 0.5 * 0.25**3
    z_up, z_down = lane < 120, lane >= 8
    inv3 = []
    for i in (1, 2):
        k = r["K3"][i]
        s = r["K3"][i - 1] + r["K3"][i + 1] + roll(k, 2, 0) + roll(k, -2, 0)
        s = s + jnp.where(z_up, roll(k, -8, 1), 0.0) + jnp.where(z_down, roll(k, 8, 1), 0.0)
        inv3.append(OMEGA / (scale3 * (6.0 * k + s)))

    lg.wait()
    all_halos(r["G"], G_CUT).wait_recv()
    planes(1, 31, 6, lambda i: [(r["V"], i, r["I0"][i] * r["G"][i])])

    far_x, far_y = row - R, slot - R
    here = (px + far_x >= 0) & (px + far_x < nx) & (py + far_y >= 0) & (py + far_y < ny)
    here = here & (far_x <= R) & (jnp.abs(far_x) + jnp.abs(far_y) <= R + 1)

    def side_copy(a, b, cyc):
        out_part = {1: slice(4, 6), -1: slice(2, 4), 0: slice(2, 6)}
        in_part = {1: slice(6, 8), -1: slice(0, 2), 0: slice(2, 6)}
        return remote(
            r["V2"].at[cyc, out_part[a], out_part[b]],
            r["VF2"].at[cyc, in_part[-a], in_part[-b]],
            S_SEM + cyc, a, b,
        )

    def row_of(a, b):
        return 8 * (b + R) + a + R

    for cyc in range(CYCLES):
        if cyc:
            all_halos(r["VB"], V_CUT).wait_recv()
            clear_edges(r["VB"], 0.0)

            def sweep(i):
                v, n = around(0, r["VB"], i)
                return [(r["V"], i, (1.0 - OMEGA) * v + r["I0"][i] * (r["G"][i] + n))]

            planes(1, 31, 3, sweep)

        def resid0(i, first=cyc == 0):
            v, n = around(0, r["V"], i)
            if first:
                return (1.0 - OMEGA) * r["G"][i] + n
            return r["G"][i] - r["T0"][i] * v + n

        planes(1, 15, 2, lambda i: [(r["S0"], i, resid0(2 * i) + resid0(2 * i + 1))])

        def start1(i):
            g = z_mean(y_pairs(r["S0"], i, 16), 0)
            return [(r["G1"], i, g), (r["V1"], i, r["I1"][i] * g)]

        planes(1, 15, 7, start1)

        def resid1(i):
            _, n = around(1, r["V1"], i)
            return (1.0 - OMEGA) * r["G1"][i] + n

        planes(1, 7, 3, lambda i: [(r["S1"], i, resid1(2 * i) + resid1(2 * i + 1))])
        v2 = r["V2"].at[cyc]
        g2 = {i: z_mean(y_pairs(r["S1"], i, 8), 1) for i in range(1, 7)}
        unrolled(1, 7, lambda i: [(v2, i, r["I2"][i] * g2[i])])

        def resid2(i):
            _, n = around(2, v2, i)
            return (1.0 - OMEGA) * g2[i] + n

        first3 = []
        for a in (0, 1):
            first3.append(inv3[a] * to_three(resid2(2 * a + 2) + resid2(2 * a + 3)))
        mine = jnp.zeros((8, 128), jnp.float32)
        for f, pair in ((0, first3), (1, [r["K3"][1], r["K3"][2]])):
            for a in (0, 1):
                for b in (0, 1):
                    mine = jnp.where(slot == 4 * f + 2 * b + a, roll(pair[a], -2 - 2 * b, 0), mine)
        near = r["C"].at[cyc]
        near[row_of(0, 0) : row_of(0, 0) + 1] = mine[0:1]
        if cyc == 0:
            pl.semaphore_wait(r["ready"], 4)
        for a, b in DIRS:
            side_copy(a, b, cyc).start()
        for a, b in PARTNERS:
            remote(
                near.at[row_of(0, 0) : row_of(0, 0) + 1],
                near.at[row_of(-a, -b) : row_of(-a, -b) + 1],
                C_SEM + cyc, a, b,
            ).start()

        rows = near.at[0 : len(PARTNERS)]
        remote(rows, rows, C_SEM + cyc, 1, 0).wait_recv()

        tiles = [near[8 * s : 8 * s + 8] for s in range(2 * R + 1)]

        def got(p):
            v = jnp.zeros((8, 128), jnp.float32)
            for s, t in enumerate(tiles):
                v = jnp.where(here & (slot == s), roll(t, s - p, 1), v)
            return v

        def sides(c, b, a):
            xp = c[b][1] if a == 0 else roll(c[b][0], -1, 0)
            xm = c[b][0] if a == 1 else roll(c[b][1], 1, 0)
            yp = c[1][a] if b == 0 else roll(c[0][a], -1, 1)
            ym = c[0][a] if b == 1 else roll(c[1][a], 1, 1)
            return xp, xm, yp, ym, roll(c[b][a], -8, 1), roll(c[b][a], 8, 1)

        if cyc == 0:
            k3 = [[got(4 + 2 * b + a) for a in (0, 1)] for b in (0, 1)]
            for b in (0, 1):
                for a in (0, 1):
                    k = k3[b][a]
                    ns = list(sides(k3, b, a))
                    ns[4] = jnp.where(z_up, ns[4], 0.0)
                    ns[5] = jnp.where(z_down, ns[5], 0.0)
                    ws = [scale3 * (k + n) for n in ns]
                    total = (ws[0] + ws[1]) + (ws[2] + ws[3]) + (ws[4] + ws[5])
                    ok = k > 0.0
                    inv = jnp.where(ok, OMEGA / jnp.where(ok, total, 1.0), 0.0)
                    ws[4] = jnp.where(z_up, ws[4], 0.0)
                    ws[5] = jnp.where(z_down, ws[5], 0.0)
                    for j, w in enumerate(ws):
                        r["W"][6 * (2 * b + a) + j] = inv * w
        start = [[got(2 * b + a) for a in (0, 1)] for b in (0, 1)]

        def coarse(_, flat):
            c = [[flat[0], flat[1]], [flat[2], flat[3]]]
            new = []
            for b in (0, 1):
                for a in (0, 1):
                    t = [r["W"][6 * (2 * b + a) + j] * n for j, n in enumerate(sides(c, b, a))]
                    v = start[b][a] + (1.0 - OMEGA) * c[b][a]
                    new.append((v + (t[0] + t[1])) + ((t[2] + t[3]) + (t[4] + t[5])))
            return tuple(new)

        flat = (start[0][0], start[0][1], start[1][0], start[1][1])
        flat = lax.fori_loop(0, SWEEPS - 1, coarse, flat)

        ring = r["VF2"].at[cyc]
        remote(ring.at[0:6], ring.at[0:6], S_SEM + cyc, 1, 0).wait_recv()
        cell = row // 2
        want = (lane & ~7) + (R - 1) + (cell + 1) // 2
        full2 = {}
        for i in range(8):
            v = ring[i]
            if 2 <= i < 6:
                v = jnp.where((row >= 2) & (row < 6), v2[i], v)
            full2[i] = jnp.where(r["K2"][i] > 0.0, v, 0.0)
        for i in range(4):
            s, a = R - 1 + (i + 1) // 2, (i + 1) % 2
            e0 = jnp.broadcast_to(flat[a][s : s + 1], (8, 128))
            e1 = jnp.broadcast_to(flat[2 + a][s : s + 1], (8, 128))
            e = jnp.take_along_axis(jnp.where(cell % 2 == 0, e1, e0), want, axis=1)
            r["VE2"][2 * i] = full2[2 * i] + e
            r["VE2"][2 * i + 1] = full2[2 * i + 1] + e

        up2 = {}
        for i in range(1, 7):
            v, n = around(2, r["VE2"], i)
            up2[i] = (1.0 - OMEGA) * v + full2[i] + r["I2"][i] * n
        for i in range(1, 7):
            r["S2"][i, pl.ds(0, 8, 2), :] = up2[i]
            r["S2"][i, pl.ds(1, 8, 2), :] = up2[i]

        unrolled(2, 14, lambda i: [(r["VE1"], i, r["V1"][i] + r["S2"][i // 2])])

        def up1(j, _):
            new = []
            for q in range(5):
                i = 3 + 5 * j + q
                v, n = around(1, r["VE1"], i)
                new.append((i, (1.0 - OMEGA) * v + r["V1"][i] + r["I1"][i] * n))
            for i, v in new:
                r["F1"][i, pl.ds(0, 16, 2), :] = v
                r["F1"][i, pl.ds(1, 16, 2), :] = v
            return 0

        lax.fori_loop(0, 2, up1, 0)

        def add0(i):
            e = r["F1"][i]
            return [(r["VE"], 2 * i + q, r["V"][2 * i + q] + e) for q in (0, 1)]

        planes(3, 13, 5, add0)

        def up0(i, c=cyc):
            v, n = around(0, r["VE"], i)
            if c == 0:
                v = (1.0 - OMEGA) * v + r["V"][i] + r["I0"][i] * n
            else:
                v = (1.0 - OMEGA) * v + r["I0"][i] * (r["G"][i] + n)
            v = v[8:24]
            if c == CYCLES - 1:
                return [(out, i - 8, v)]
            return [(r["VB"].at[:, 8:24], i, v), (r["F0"], i - 8, v)]

        planes(8, 24, 4, up0)
        if cyc < CYCLES - 1:
            send_halo(r["F0"], r["VB"], V_SEM, V_CUT)

    all_halos(r["M"], H).wait_send()
    all_halos(r["G"], G_CUT).wait_send()
    all_halos(r["VB"], V_CUT).wait_send()
    for cyc in range(CYCLES):
        ring = r["VF2"].at[cyc, 0:6]
        remote(ring, ring, S_SEM + cyc, 1, 0).wait_send()
        rows = r["C"].at[cyc, 0 : len(PARTNERS)]
        remote(rows, rows, C_SEM + cyc, 1, 0).wait_send()


M_SEM, G_SEM, V_SEM, S_SEM, C_SEM = 0, 1, 2, 3, 3 + CYCLES


def scratch():
    f = jnp.float32

    def vm(*shape):
        return pltpu.VMEM(shape, f)

    a, b, c = vm(32, 32, 128), vm(16, 16, 128), vm(8, 8, 128)
    dma = pltpu.SemaphoreType.DMA
    shapes = [a, pltpu.VMEM((32, 32, 128), jnp.int32)] + [a] * 9
    shapes += [vm(16, 32, 128)] * 2 + [b] * 8 + [vm(8, 16, 128)] * 2
    shapes += [c] + [vm(CYCLES, 8, 8, 128)] * 2 + [c] * 5 + [vm(4, 8, 128), b]
    shapes += [vm(CYCLES, 64, 128), vm(24, 8, 128)]
    sems = C_SEM + CYCLES
    return shapes + [dma((2,)), dma((sems,)), dma((sems,)), pltpu.SemaphoreType.REGULAR]


def local(right_side, material, conductivity):
    nx, ny = lax.axis_size("gx"), lax.axis_size("gy")
    return pl.pallas_call(
        functools.partial(kernel, nx, ny),
        out_shape=jax.ShapeDtypeStruct(right_side.shape, right_side.dtype),
        in_specs=[
            pl.BlockSpec(memory_space=pltpu.SMEM),
            pl.BlockSpec(memory_space=pl.ANY),
            pl.BlockSpec(memory_space=pl.ANY),
        ],
        out_specs=pl.BlockSpec(memory_space=pltpu.VMEM),
        scratch_shapes=scratch(),
        compiler_params=pltpu.CompilerParams(collective_id=0, has_side_effects=True),
        name="vcycles",
    )(conductivity, right_side, material)


def solution(mesh):
    return jax.shard_map(
        local,
        mesh=mesh,
        in_specs=(P("gx", "gy", None), P("gx", "gy", None), P()),
        out_specs=P("gx", "gy", None),
        check_vma=False,
    )
```

time: 532 us -> 49.5 us (0.09); the launches traced: 522 us -> 49.4 us
  starting transfers between devices: 314 us -> 0 us
  waiting for transfers between devices: 119 us -> 0 us
  Pallas kernels: 0 us -> 47.8 us
  other arithmetic: 43.6 us -> 0 us
  local copies, waits for them, and re-layouts: 42.3 us -> 1.57 us
    ppermute x91 -> x0, starting transfers between devices: 314 us -> none  [the longest x27 136 us: partner(): return lax.ppermute(block, axis, route)]
    ppermute x91 -> x0, waiting for transfers between devices: 119 us -> none  [the longest x32 78.8 us: extended(): after = lax.ppermute(first, axis, down)]
    pallas_call x0 -> x1, Pallas kernels: none -> 47.8 us  [local(): pl.pallas_call(functools.partial(kernel, nx, ny), out_shape=jax.ShapeDtyp...]
    reshape x19 -> x0, local copies, waits for them, and re-layouts: 36.1 us -> none  [the longest x7 32.4 us: restrict(): field.reshape(sx // 2, 2, sy // 2, 2, sz // 2, 2).mean(axis=(1, 3, 5))]
    reduce_sum x9 -> x0, other arithmetic: 13.5 us -> none  [restrict(): field.reshape(sx // 2, 2, sy // 2, 2, sz // 2, 2).mean(axis=(1, 3, 5))]
    select_n x26 -> x0, other arithmetic: 11.5 us -> none  [the longest x1 11.1 us: local(): cond = jnp.where(material == which, conductivity[which], cond)]
    add x23 -> x0, other arithmetic: 11 us -> none  [the longest x7 6.73 us: cycle(): field + OMEGA * (right - apply_operator(field_pad(field), faces, total))...]
  transfers between devices with their start and end apart: 91 -> 0, of which waited for: 37 -> 0; matrix products, arithmetic and copies ran while one was open for 6% -> 0% of each run, Pallas kernels for 0% -> 0%
where the time goes in v2:
time: 49.5 us; the launch traced here: 49.4 us
  Pallas kernels  47.8 us (97%)
  local copies, waits for them, and re-layouts  1.57 us (3%)
    pallas_call x1, Pallas kernels, local(): pl.pallas_call(functools.partial(kernel, nx, ny), out_shape=jax.ShapeDtyp...  47.8 us
    unnamed x1, local copies, waits for them, and re-layouts  1.57 us

profile of v2, /device:TPU:1, one launch (start us, length us, event | category | flops | bytes accessed | tf_op | source)
XLA Modules:
  0.0 49.4 jit_solution(11510847721544456383)
XLA Ops:
  0.0 47.8 %vcycles.1 = f32[16,16,128]{2,1,0:T(8,128)} custom-call(f32[16]{0:T(128)} %cond.1, f32[16,16,128]{2,1,0:T(8,128)} %g_hbm.1, s32[16,16,128]{2,1,0:T(8,128)} %m_hbm.1), custom_call_target="tpu_custom_call" | custom-call | tf_op jit(solution)/shard_map/vcycles/pallas_call | solution.py:437
  47.8 1.6 %copy.5 = f32[16,16,128]{2,1,0:T(8,128)} copy(f32[16,16,128]{2,1,0:T(8,128)} %vcycles.1) | data formatting | bytes 262144

commit v3 on v2

--- a/solution.py
+++ b/solution.py
@@ -24,7 +24,6 @@
         key=lambda d: -abs(d[0]) - 1.25 * abs(d[1]),
     )
 )
-G_CUT, V_CUT = 6, 7
 
 
 def send_part(s, n=H):
@@ -53,21 +52,44 @@
         "G", "M", "K0", "V", "VB", "VE", "I0", "T0", "X0", "Y0", "Z0", "S0", "F1",
         "K1", "V1", "G1", "VE1", "I1", "X1", "Y1", "Z1", "S1", "S2",
         "K2", "V2", "VF2", "VE2", "I2", "X2", "Y2", "Z2", "K3", "F0", "C", "W",
-        "lsem", "send", "recv", "ready",
+        "FM", "FZ", "MS", "GS", "VS", "RS", "CS", "lsem", "send", "recv", "ready",
     )
     r = dict(zip(names, refs, strict=True))
     px, py = lax.axis_index("gx"), lax.axis_index("gy")
-    xs = {d: lax.rem(px + (d + nx), nx) if d else px for d in STEPS}
-    ys = {d: lax.rem(py + (d + ny), ny) if d else py for d in STEPS}
-
-    def dev(a, b):
-        return (xs[a], ys[b])
+    x_ok = {d: (px + d >= 0) & (px + d < nx) for d in STEPS}
+    y_ok = {d: (py + d >= 0) & (py + d < ny) for d in STEPS}
+
+    def exists(a, b):
+        if a == 0:
+            return y_ok[b]
+        return x_ok[a] if b == 0 else x_ok[a] & y_ok[b]
 
     def remote(src, dst, sem, a, b):
         return pltpu.make_async_remote_copy(
             src_ref=src, dst_ref=dst, send_sem=r["send"].at[sem], recv_sem=r["recv"].at[sem],
-            device_id=dev(a, b), device_id_type=MESH,
+            device_id=(px + a, py + b), device_id_type=MESH,
         )
+
+    def push(src, dst, sem, a, b, hole, fill, spare):
+        ok = exists(a, b)
+        pl.when(ok)(lambda: remote(src, dst, sem, a, b).start())
+
+        @pl.when(jnp.logical_not(ok))
+        def _():
+            pltpu.make_async_copy(fill, hole, r["recv"].at[sem]).start()
+            pltpu.make_async_copy(fill, spare, r["send"].at[sem]).start()
+
+    def tell(sem, sides):
+        for a, b in sides:
+            @pl.when(exists(a, b))
+            def _(a=a, b=b):
+                pl.semaphore_signal(sem, inc=1, device_id=(px + a, py + b), device_id_type=MESH)
+
+    def count(sides):
+        n = jnp.int32(0)
+        for a, b in sides:
+            n = n + jnp.where(exists(a, b), 1, 0)
+        return n
 
     own = (slice(8, 24), slice(8, 24))
     lg = pltpu.make_async_copy(g_hbm, r["G"].at[own], r["lsem"].at[0])
@@ -75,8 +97,9 @@
     lm.start()
     lg.start()
     barrier = pltpu.get_barrier_semaphore()
-    for a, b in DIRS:
-        pl.semaphore_signal(barrier, inc=1, device_id=dev(a, b), device_id_type=MESH)
+    tell(barrier, FOUR)
+    r["FM"][...] = jnp.full((16, 16, 128), NMAT, jnp.int32)
+    r["FZ"][...] = jnp.zeros((16, 16, 128), jnp.float32)
     lane = iota((8, 128), 1)
     row = iota((8, 128), 0)
     slot = lane & 7
@@ -84,51 +107,47 @@
     for i in range(NMAT):
         table = jnp.where(lane == i, cond[i], table)
     table32 = jnp.concatenate([table] * 4, 0)
-    pl.semaphore_wait(barrier, len(DIRS))
-
-    def send_halo(src, dst, sem, cut):
-        for a, b in DIRS:
-            n = cut if a and b else H
-            remote(
-                src.at[send_part(a, n), send_part(b)],
-                dst.at[halo_part(-a, n), halo_part(-b)],
-                sem, a, b,
-            ).start()
-
-    def all_halos(dst, cut):
-        view = dst.at[0 : (512 + 4 * H * cut) // 32]
-        sem = {"M": M_SEM, "G": G_SEM, "VB": V_SEM}
-        for name in sem:
-            if dst is r[name]:
-                return remote(view, view, sem[name], 1, 0)
-        raise ValueError
-
-    def clear_edges(ref, value):
-        full = functools.partial(jnp.full, fill_value=value, dtype=ref.dtype)
-
-        @pl.when(px == 0)
-        def _():
-            ref[0:8] = full((8, 32, 128))
-
-        @pl.when(px == nx - 1)
-        def _():
-            ref[24:32] = full((8, 32, 128))
-
-        @pl.when(py == 0)
-        def _():
-            ref[:, 0:8] = full((32, 8, 128))
-
-        @pl.when(py == ny - 1)
-        def _():
-            ref[:, 24:32] = full((32, 8, 128))
-
-    send_halo(m_hbm, r["M"], M_SEM, H)
-    send_halo(g_hbm, r["G"], G_SEM, G_CUT)
+    pl.semaphore_wait(barrier, count(FOUR))
+
+    def send_faces(src, name, along_y):
+        dst, fill, spare, sem = r[name], r[FILL[name]], r[SPARE[name]], SEM[name]
+        for q in (1, -1):
+            a, b = (0, q) if along_y else (q, 0)
+            hole = (halo_part(a), halo_part(b))
+            push(
+                src.at[send_part(a), send_part(b)], dst.at[halo_part(-a), halo_part(-b)],
+                sem if along_y else sem + 1, a, b,
+                dst.at[hole], fill.at[0 : 8 if a else 16, 0 : 8 if b else 16], spare.at[hole],
+            )
+
+    def send_corners(name):
+        dst, fill, spare, n = r[name], r[FILL[name]], r[SPARE[name]], CUT[name]
+        for a in (1, -1):
+            near_planes = slice(24 - n, 24) if a == 1 else slice(8, 8 + n)
+            for b in (1, -1):
+                hole = (halo_part(a, n), halo_part(b))
+                push(
+                    dst.at[near_planes, halo_part(b)], dst.at[halo_part(-a, n), halo_part(b)],
+                    SEM[name] + 1, a, 0, dst.at[hole], fill.at[0:n, 0:8], spare.at[hole],
+                )
+
+    def y_faces(name):
+        view = r[name].at[0:8]
+        return remote(view, view, SEM[name], 1, 0)
+
+    def the_rest(name):
+        view = r[name].at[0 : 8 + CUT[name]]
+        return remote(view, view, SEM[name] + 1, 1, 0)
+
+    send_faces(m_hbm, "M", True)
+    send_faces(m_hbm, "M", False)
+    send_faces(g_hbm, "G", True)
+    y_faces("M").wait_recv()
+    send_corners("M")
+    send_faces(g_hbm, "G", False)
     lm.wait()
-    all_halos(r["M"], H).wait_recv()
-    for a, b in ((-1, 0), (1, 0), (0, -1), (0, 1)):
-        pl.semaphore_signal(r["ready"], inc=1, device_id=dev(a, b), device_id_type=MESH)
-    clear_edges(r["M"], NMAT)
+    the_rest("M").wait_recv()
+    tell(r["ready"], FOUR)
 
     def planes(lo, hi, step, one):
         def body(j, _):
@@ -200,6 +219,8 @@
     unrolled(0, 4, lambda i: [(r["K3"], i, to_three(r["K2"][2 * i] + r["K2"][2 * i + 1]))])
     for lv, scale in ((0, 0.5), (1, 0.125), (2, 0.03125)):
         r[f"X{lv}"][0] = scale * (r[f"K{lv}"][0] + r[f"K{lv}"][1])
+    y_faces("G").wait_recv()
+    send_corners("G")
     planes(1, 31, 3, functools.partial(face_values, 0))
     planes(1, 15, 7, functools.partial(face_values, 1))
     unrolled(1, 7, functools.partial(face_values, 2))
@@ -214,7 +235,7 @@
         inv3.append(OMEGA / (scale3 * (6.0 * k + s)))
 
     lg.wait()
-    all_halos(r["G"], G_CUT).wait_recv()
+    the_rest("G").wait_recv()
     planes(1, 31, 6, lambda i: [(r["V"], i, r["I0"][i] * r["G"][i])])
 
     far_x, far_y = row - R, slot - R
@@ -224,10 +245,10 @@
     def side_copy(a, b, cyc):
         out_part = {1: slice(4, 6), -1: slice(2, 4), 0: slice(2, 6)}
         in_part = {1: slice(6, 8), -1: slice(0, 2), 0: slice(2, 6)}
-        return remote(
-            r["V2"].at[cyc, out_part[a], out_part[b]],
-            r["VF2"].at[cyc, in_part[-a], in_part[-b]],
-            S_SEM + cyc, a, b,
+        src, hole = (cyc, out_part[a], out_part[b]), (cyc, in_part[a], in_part[b])
+        push(
+            r["V2"].at[src], r["VF2"].at[cyc, in_part[-a], in_part[-b]], S_SEM + cyc, a, b,
+            r["VF2"].at[hole], r["V2"].at[src], r["RS"].at[hole],
         )
 
     def row_of(a, b):
@@ -235,8 +256,9 @@
 
     for cyc in range(CYCLES):
         if cyc:
-            all_halos(r["VB"], V_CUT).wait_recv()
-            clear_edges(r["VB"], 0.0)
+            y_faces("VB").wait_recv()
+            send_corners("VB")
+            the_rest("VB").wait_recv()
 
             def sweep(i):
                 v, n = around(0, r["VB"], i)
@@ -282,15 +304,16 @@
         near = r["C"].at[cyc]
         near[row_of(0, 0) : row_of(0, 0) + 1] = mine[0:1]
         if cyc == 0:
-            pl.semaphore_wait(r["ready"], 4)
+            pl.semaphore_wait(r["ready"], count(FOUR))
         for a, b in DIRS:
-            side_copy(a, b, cyc).start()
+            side_copy(a, b, cyc)
+        my_row = near.at[row_of(0, 0) : row_of(0, 0) + 1]
         for a, b in PARTNERS:
-            remote(
-                near.at[row_of(0, 0) : row_of(0, 0) + 1],
-                near.at[row_of(-a, -b) : row_of(-a, -b) + 1],
-                C_SEM + cyc, a, b,
-            ).start()
+            there, hole = row_of(-a, -b), row_of(a, b)
+            push(
+                my_row, near.at[there : there + 1], C_SEM + cyc, a, b,
+                near.at[hole : hole + 1], my_row, r["CS"].at[cyc, hole : hole + 1],
+            )
 
         rows = near.at[0 : len(PARTNERS)]
         remote(rows, rows, C_SEM + cyc, 1, 0).wait_recv()
@@ -401,11 +424,12 @@
 
         planes(8, 24, 4, up0)
         if cyc < CYCLES - 1:
-            send_halo(r["F0"], r["VB"], V_SEM, V_CUT)
-
-    all_halos(r["M"], H).wait_send()
-    all_halos(r["G"], G_CUT).wait_send()
-    all_halos(r["VB"], V_CUT).wait_send()
+            send_faces(r["F0"], "VB", True)
+            send_faces(r["F0"], "VB", False)
+
+    for name in SEM:
+        y_faces(name).wait_send()
+        the_rest(name).wait_send()
     for cyc in range(CYCLES):
         ring = r["VF2"].at[cyc, 0:6]
         remote(ring, ring, S_SEM + cyc, 1, 0).wait_send()
@@ -413,7 +437,12 @@
         remote(rows, rows, C_SEM + cyc, 1, 0).wait_send()
 
 
-M_SEM, G_SEM, V_SEM, S_SEM, C_SEM = 0, 1, 2, 3, 3 + CYCLES
+SEM = {"M": 0, "G": 2, "VB": 4}
+S_SEM, C_SEM = 6, 6 + CYCLES
+CUT = {"M": 8, "G": 6, "VB": 7}
+FILL = {"M": "FM", "G": "FZ", "VB": "FZ"}
+SPARE = {"M": "MS", "G": "GS", "VB": "VS"}
+FOUR = ((1, 0), (-1, 0), (0, 1), (0, -1))
 
 
 def scratch():
@@ -429,6 +458,8 @@
     shapes += [c] + [vm(CYCLES, 8, 8, 128)] * 2 + [c] * 5 + [vm(4, 8, 128), b]
     shapes += [vm(CYCLES, 64, 128), vm(24, 8, 128)]
     sems = C_SEM + CYCLES
+    i16, i32 = (pltpu.VMEM((n, n, 128), jnp.int32) for n in (16, 32))
+    shapes += [i16, b, i32, a, a, vm(CYCLES, 8, 8, 128), vm(CYCLES, 64, 128)]
     return shapes + [dma((2,)), dma((sems,)), dma((sems,)), pltpu.SemaphoreType.REGULAR]
 
 

time: 49.5 us -> 50.2 us (1.014)
  the two profiles are of different devices: /device:TPU:1 before, /device:TPU:6 now
where the time goes in v3:
time: 50.2 us; the launch traced here: 50.1 us
  Pallas kernels  48.5 us (97%)
  local copies, waits for them, and re-layouts  1.57 us (3%)
    pallas_call x1, Pallas kernels, local(): pl.pallas_call(functools.partial(kernel, nx, ny), out_shape=jax.ShapeDtyp...  48.5 us
    unnamed x1, local copies, waits for them, and re-layouts  1.57 us

profile of v3, /device:TPU:6, one launch (start us, length us, event | category | flops | bytes accessed | tf_op | source)
XLA Modules:
  0.0 50.1 jit_solution(9334087768197642927)
XLA Ops:
  0.0 48.5 %vcycles.1 = f32[16,16,128]{2,1,0:T(8,128)} custom-call(f32[16]{0:T(128)} %cond.1, f32[16,16,128]{2,1,0:T(8,128)} %g_hbm.1, s32[16,16,128]{2,1,0:T(8,128)} %m_hbm.1), custom_call_target="tpu_custom_call" | custom-call | tf_op jit(solution)/shard_map/vcycles/pallas_call | solution.py:468
  48.5 1.6 %copy.5 = f32[16,16,128]{2,1,0:T(8,128)} copy(f32[16,16,128]{2,1,0:T(8,128)} %vcycles.1) | data formatting | bytes 262144

commit v4 on v3

--- a/solution.py
+++ b/solution.py
@@ -52,13 +52,16 @@
         "G", "M", "K0", "V", "VB", "VE", "I0", "T0", "X0", "Y0", "Z0", "S0", "F1",
         "K1", "V1", "G1", "VE1", "I1", "X1", "Y1", "Z1", "S1", "S2",
         "K2", "V2", "VF2", "VE2", "I2", "X2", "Y2", "Z2", "K3", "F0", "C", "W",
-        "FM", "FZ", "MS", "GS", "VS", "RS", "CS", "lsem", "send", "recv", "ready",
+        "FM", "FZ", "MS", "GS", "VS", "lsem", "send", "recv", "ready",
     )
     r = dict(zip(names, refs, strict=True))
     px, py = lax.axis_index("gx"), lax.axis_index("gy")
     x_ok = {d: (px + d >= 0) & (px + d < nx) for d in STEPS}
     y_ok = {d: (py + d >= 0) & (py + d < ny) for d in STEPS}
 
+    xs = {d: lax.rem(px + (d + nx), nx) if d else px for d in STEPS}
+    ys = {d: lax.rem(py + (d + ny), ny) if d else py for d in STEPS}
+
     def exists(a, b):
         if a == 0:
             return y_ok[b]
@@ -67,7 +70,7 @@
     def remote(src, dst, sem, a, b):
         return pltpu.make_async_remote_copy(
             src_ref=src, dst_ref=dst, send_sem=r["send"].at[sem], recv_sem=r["recv"].at[sem],
-            device_id=(px + a, py + b), device_id_type=MESH,
+            device_id=(xs[a], ys[b]), device_id_type=MESH,
         )
 
     def push(src, dst, sem, a, b, hole, fill, spare):
@@ -79,17 +82,9 @@
             pltpu.make_async_copy(fill, hole, r["recv"].at[sem]).start()
             pltpu.make_async_copy(fill, spare, r["send"].at[sem]).start()
 
-    def tell(sem, sides):
-        for a, b in sides:
-            @pl.when(exists(a, b))
-            def _(a=a, b=b):
-                pl.semaphore_signal(sem, inc=1, device_id=(px + a, py + b), device_id_type=MESH)
-
-    def count(sides):
-        n = jnp.int32(0)
-        for a, b in sides:
-            n = n + jnp.where(exists(a, b), 1, 0)
-        return n
+    def tell(sem):
+        for a, b in FOUR:
+            pl.semaphore_signal(sem, inc=1, device_id=(xs[a], ys[b]), device_id_type=MESH)
 
     own = (slice(8, 24), slice(8, 24))
     lg = pltpu.make_async_copy(g_hbm, r["G"].at[own], r["lsem"].at[0])
@@ -97,7 +92,7 @@
     lm.start()
     lg.start()
     barrier = pltpu.get_barrier_semaphore()
-    tell(barrier, FOUR)
+    tell(barrier)
     r["FM"][...] = jnp.full((16, 16, 128), NMAT, jnp.int32)
     r["FZ"][...] = jnp.zeros((16, 16, 128), jnp.float32)
     lane = iota((8, 128), 1)
@@ -107,7 +102,8 @@
     for i in range(NMAT):
         table = jnp.where(lane == i, cond[i], table)
     table32 = jnp.concatenate([table] * 4, 0)
-    pl.semaphore_wait(barrier, count(FOUR))
+    pl.semaphore_wait(barrier, 4)
+    tell(r["ready"].at[0])
 
     def send_faces(src, name, along_y):
         dst, fill, spare, sem = r[name], r[FILL[name]], r[SPARE[name]], SEM[name]
@@ -131,6 +127,22 @@
                     SEM[name] + 1, a, 0, dst.at[hole], fill.at[0:n, 0:8], spare.at[hole],
                 )
 
+    def send_field():
+        dst, n = r["VB"], CUT["VB"]
+        for a, b in sorted(DIRS, key=lambda d: -abs(d[0]) - abs(d[1])):
+            m = n if a and b else H
+            hole = (halo_part(a, m), halo_part(b))
+            tall, wide = m if a else 16, 8 if b else 16
+            push(
+                r["F0"].at[send_part(a, m), send_part(b)],
+                dst.at[halo_part(-a, m), halo_part(-b)], V_SEM, a, b,
+                dst.at[hole], r["FZ"].at[0:tall, 0:wide], r["VS"].at[hole],
+            )
+
+    def field():
+        view = r["VB"].at[0 : 16 + CUT["VB"]]
+        return remote(view, view, V_SEM, 1, 0)
+
     def y_faces(name):
         view = r[name].at[0:8]
         return remote(view, view, SEM[name], 1, 0)
@@ -145,9 +157,12 @@
     y_faces("M").wait_recv()
     send_corners("M")
     send_faces(g_hbm, "G", False)
+    pl.semaphore_wait(r["ready"].at[0], 4)
+    tell(r["ready"].at[1])
     lm.wait()
     the_rest("M").wait_recv()
-    tell(r["ready"], FOUR)
+    pl.semaphore_wait(r["ready"].at[1], 4)
+    tell(r["ready"].at[2])
 
     def planes(lo, hi, step, one):
         def body(j, _):
@@ -245,10 +260,10 @@
     def side_copy(a, b, cyc):
         out_part = {1: slice(4, 6), -1: slice(2, 4), 0: slice(2, 6)}
         in_part = {1: slice(6, 8), -1: slice(0, 2), 0: slice(2, 6)}
-        src, hole = (cyc, out_part[a], out_part[b]), (cyc, in_part[a], in_part[b])
-        push(
-            r["V2"].at[src], r["VF2"].at[cyc, in_part[-a], in_part[-b]], S_SEM + cyc, a, b,
-            r["VF2"].at[hole], r["V2"].at[src], r["RS"].at[hole],
+        return remote(
+            r["V2"].at[cyc, out_part[a], out_part[b]],
+            r["VF2"].at[cyc, in_part[-a], in_part[-b]],
+            S_SEM + cyc, a, b,
         )
 
     def row_of(a, b):
@@ -256,9 +271,7 @@
 
     for cyc in range(CYCLES):
         if cyc:
-            y_faces("VB").wait_recv()
-            send_corners("VB")
-            the_rest("VB").wait_recv()
+            field().wait_recv()
 
             def sweep(i):
                 v, n = around(0, r["VB"], i)
@@ -304,16 +317,13 @@
         near = r["C"].at[cyc]
         near[row_of(0, 0) : row_of(0, 0) + 1] = mine[0:1]
         if cyc == 0:
-            pl.semaphore_wait(r["ready"], count(FOUR))
+            pl.semaphore_wait(r["ready"].at[2], 4)
         for a, b in DIRS:
-            side_copy(a, b, cyc)
+            side_copy(a, b, cyc).start()
         my_row = near.at[row_of(0, 0) : row_of(0, 0) + 1]
         for a, b in PARTNERS:
-            there, hole = row_of(-a, -b), row_of(a, b)
-            push(
-                my_row, near.at[there : there + 1], C_SEM + cyc, a, b,
-                near.at[hole : hole + 1], my_row, r["CS"].at[cyc, hole : hole + 1],
-            )
+            there = row_of(-a, -b)
+            remote(my_row, near.at[there : there + 1], C_SEM + cyc, a, b).start()
 
         rows = near.at[0 : len(PARTNERS)]
         remote(rows, rows, C_SEM + cyc, 1, 0).wait_recv()
@@ -424,12 +434,12 @@
 
         planes(8, 24, 4, up0)
         if cyc < CYCLES - 1:
-            send_faces(r["F0"], "VB", True)
-            send_faces(r["F0"], "VB", False)
+            send_field()
 
     for name in SEM:
         y_faces(name).wait_send()
         the_rest(name).wait_send()
+    field().wait_send()
     for cyc in range(CYCLES):
         ring = r["VF2"].at[cyc, 0:6]
         remote(ring, ring, S_SEM + cyc, 1, 0).wait_send()
@@ -437,11 +447,11 @@
         remote(rows, rows, C_SEM + cyc, 1, 0).wait_send()
 
 
-SEM = {"M": 0, "G": 2, "VB": 4}
-S_SEM, C_SEM = 6, 6 + CYCLES
+SEM = {"M": 0, "G": 2}
+V_SEM, S_SEM, C_SEM = 4, 5, 5 + CYCLES
 CUT = {"M": 8, "G": 6, "VB": 7}
-FILL = {"M": "FM", "G": "FZ", "VB": "FZ"}
-SPARE = {"M": "MS", "G": "GS", "VB": "VS"}
+FILL = {"M": "FM", "G": "FZ"}
+SPARE = {"M": "MS", "G": "GS"}
 FOUR = ((1, 0), (-1, 0), (0, 1), (0, -1))
 
 
@@ -459,8 +469,8 @@
     shapes += [vm(CYCLES, 64, 128), vm(24, 8, 128)]
     sems = C_SEM + CYCLES
     i16, i32 = (pltpu.VMEM((n, n, 128), jnp.int32) for n in (16, 32))
-    shapes += [i16, b, i32, a, a, vm(CYCLES, 8, 8, 128), vm(CYCLES, 64, 128)]
-    return shapes + [dma((2,)), dma((sems,)), dma((sems,)), pltpu.SemaphoreType.REGULAR]
+    shapes += [i16, b, i32, a, a]
+    return shapes + [dma((2,)), dma((sems,)), dma((sems,)), pltpu.SemaphoreType.REGULAR((3,))]
 
 
 def local(right_side, material, conductivity):

time: 50.2 us -> 48.9 us (0.974)
  the two profiles are of different devices: /device:TPU:6 before, /device:TPU:1 now
where the time goes in v4:
time: 48.9 us; the launch traced here: 48.1 us
  Pallas kernels  46.5 us (95%)
  local copies, waits for them, and re-layouts  1.57 us (3%)
    pallas_call x1, Pallas kernels, local(): pl.pallas_call(functools.partial(kernel, nx, ny), out_shape=jax.ShapeDtyp...  46.5 us
    unnamed x1, local copies, waits for them, and re-layouts  1.57 us

profile of v4, /device:TPU:1, one launch (start us, length us, event | category | flops | bytes accessed | tf_op | source)
XLA Modules:
  0.0 48.1 jit_solution(4535305723502185166)
XLA Ops:
  0.0 46.5 %vcycles.1 = f32[16,16,128]{2,1,0:T(8,128)} custom-call(f32[16]{0:T(128)} %cond.1, f32[16,16,128]{2,1,0:T(8,128)} %g_hbm.1, s32[16,16,128]{2,1,0:T(8,128)} %m_hbm.1), custom_call_target="tpu_custom_call" | custom-call | tf_op jit(solution)/shard_map/vcycles/pallas_call | solution.py:478
  46.5 1.6 %copy.5 = f32[16,16,128]{2,1,0:T(8,128)} copy(f32[16,16,128]{2,1,0:T(8,128)} %vcycles.1) | data formatting | bytes 262144

commit v5 on v4

--- a/solution.py
+++ b/solution.py
@@ -160,9 +160,6 @@
     pl.semaphore_wait(r["ready"].at[0], 4)
     tell(r["ready"].at[1])
     lm.wait()
-    the_rest("M").wait_recv()
-    pl.semaphore_wait(r["ready"].at[1], 4)
-    tell(r["ready"].at[2])
 
     def planes(lo, hi, step, one):
         def body(j, _):
@@ -195,7 +192,7 @@
         s = s + jnp.where(below, kz, 0.0) + jnp.where(above, roll(k, step, 1), 0.0)
         total = scale * s
         inside = k > 0.0
-        inv = jnp.where(inside, OMEGA / jnp.where(inside, total, 1.0), 0.0)
+        inv = jnp.where(inside, OMEGA / total, 0.0)
         res = [
             (r[f"X{lv}"], i, scale * (k + kn)),
             (r[f"Y{lv}"], i, scale * (k + ky)),
@@ -227,16 +224,29 @@
         k = [jnp.take_along_axis(table32, r["M"][2 * i + q], axis=1) for q in (0, 1)]
         return [(r["K0"], 2 * i, k[0]), (r["K0"], 2 * i + 1, k[1]), (r["S0"], i, k[0] + k[1])]
 
-    planes(0, 16, 4, look)
-    planes(0, 16, 8, lambda i: [(r["K1"], i, z_mean(y_pairs(r["S0"], i, 16), 0))])
+    def mean1(i):
+        return [(r["K1"], i, z_mean(y_pairs(r["S0"], i, 16), 0))]
+
+    faces0 = functools.partial(face_values, 0)
+    planes(4, 12, 4, look)
+    y_faces("G").wait_recv()
+    send_corners("G")
+    planes(4, 12, 8, mean1)
+    planes(9, 23, 2, faces0)
+    the_rest("M").wait_recv()
+    pl.semaphore_wait(r["ready"].at[1], 4)
+    tell(r["ready"].at[2])
+    planes(0, 4, 4, look)
+    planes(12, 16, 4, look)
+    planes(0, 4, 4, mean1)
+    planes(12, 16, 4, mean1)
     unrolled(0, 8, lambda i: [(r["S1"], i, r["K1"][2 * i] + r["K1"][2 * i + 1])])
     unrolled(0, 8, lambda i: [(r["K2"], i, z_mean(y_pairs(r["S1"], i, 8), 1))])
     unrolled(0, 4, lambda i: [(r["K3"], i, to_three(r["K2"][2 * i] + r["K2"][2 * i + 1]))])
     for lv, scale in ((0, 0.5), (1, 0.125), (2, 0.03125)):
         r[f"X{lv}"][0] = scale * (r[f"K{lv}"][0] + r[f"K{lv}"][1])
-    y_faces("G").wait_recv()
-    send_corners("G")
-    planes(1, 31, 3, functools.partial(face_values, 0))
+    planes(1, 9, 4, faces0)
+    planes(23, 31, 4, faces0)
     planes(1, 15, 7, functools.partial(face_values, 1))
     unrolled(1, 7, functools.partial(face_values, 2))
 
@@ -477,7 +487,7 @@
     nx, ny = lax.axis_size("gx"), lax.axis_size("gy")
     return pl.pallas_call(
         functools.partial(kernel, nx, ny),
-        out_shape=jax.ShapeDtypeStruct(right_side.shape, right_side.dtype),
+        out_shape=pltpu.VMEM(right_side.shape, right_side.dtype),
         in_specs=[
             pl.BlockSpec(memory_space=pltpu.SMEM),
             pl.BlockSpec(memory_space=pl.ANY),

time: 48.9 us -> 45.6 us (0.933); the launches traced: 48.1 us -> 45.4 us
  Pallas kernels: 46.5 us -> 44.8 us
  local copies, waits for them, and re-layouts: 1.57 us -> 0.66 us
    pallas_call x1, Pallas kernels: 46.5 us -> 44.8 us  [local(): pl.pallas_call(functools.partial(kernel, nx, ny), out_shape=pltpu.VMEM(ri...]
    unnamed x1, local copies, waits for them, and re-layouts: 1.57 us -> 0.66 us
where the time goes in v5:
time: 45.6 us; the launch traced here: 45.4 us
  Pallas kernels  44.8 us (98%)
  local copies, waits for them, and re-layouts  0.66 us (1%)
    pallas_call x1, Pallas kernels, local(): pl.pallas_call(functools.partial(kernel, nx, ny), out_shape=pltpu.VMEM(ri...  44.8 us

profile of v5, /device:TPU:1, one launch (start us, length us, event | category | flops | bytes accessed | tf_op | source)
XLA Modules:
  0.0 45.4 jit_solution(6056998376937617999)
XLA Ops:
  0.0 44.8 %vcycles.1 = f32[16,16,128]{2,1,0:T(8,128)S(1)} custom-call(f32[16]{0:T(128)} %cond.1, f32[16,16,128]{2,1,0:T(8,128)} %g_hbm.1, s32[16,16,128]{2,1,0:T(8,128)} %m_hbm.1), custom_call_target="tpu_custom_call" | custom-call | tf_op jit(solution)/shard_map/vcycles/pallas_call | solution.py:488
  44.8 0.7 %copy.5 = f32[16,16,128]{2,1,0:T(8,128)} copy(f32[16,16,128]{2,1,0:T(8,128)S(1)} %vcycles.1) | data formatting | bytes 262144

commit v6 on v5

--- a/solution.py
+++ b/solution.py
@@ -129,19 +129,19 @@
 
     def send_field():
         dst, n = r["VB"], CUT["VB"]
-        for a, b in sorted(DIRS, key=lambda d: -abs(d[0]) - abs(d[1])):
+        for a, b in sorted(DIRS, key=lambda d: (abs(d[0]), -abs(d[1]))):
             m = n if a and b else H
             hole = (halo_part(a, m), halo_part(b))
             tall, wide = m if a else 16, 8 if b else 16
             push(
                 r["F0"].at[send_part(a, m), send_part(b)],
-                dst.at[halo_part(-a, m), halo_part(-b)], V_SEM, a, b,
+                dst.at[halo_part(-a, m), halo_part(-b)], V_SEM + abs(a), a, b,
                 dst.at[hole], r["FZ"].at[0:tall, 0:wide], r["VS"].at[hole],
             )
 
-    def field():
-        view = r["VB"].at[0 : 16 + CUT["VB"]]
-        return remote(view, view, V_SEM, 1, 0)
+    def field(rest):
+        view = r["VB"].at[0 : 8 + CUT["VB"] if rest else 8]
+        return remote(view, view, V_SEM + rest, 1, 0)
 
     def y_faces(name):
         view = r[name].at[0:8]
@@ -281,13 +281,13 @@
 
     for cyc in range(CYCLES):
         if cyc:
-            field().wait_recv()
 
             def sweep(i):
                 v, n = around(0, r["VB"], i)
                 return [(r["V"], i, (1.0 - OMEGA) * v + r["I0"][i] * (r["G"][i] + n))]
 
-            planes(1, 31, 3, sweep)
+            field(0).wait_recv()
+            planes(9, 23, 2, sweep)
 
         def resid0(i, first=cyc == 0):
             v, n = around(0, r["V"], i)
@@ -295,7 +295,18 @@
                 return (1.0 - OMEGA) * r["G"][i] + n
             return r["G"][i] - r["T0"][i] * v + n
 
-        planes(1, 15, 2, lambda i: [(r["S0"], i, resid0(2 * i) + resid0(2 * i + 1))])
+        def down0(i):
+            return [(r["S0"], i, resid0(2 * i) + resid0(2 * i + 1))]
+
+        if cyc:
+            planes(5, 11, 2, down0)
+            field(1).wait_recv()
+            planes(1, 9, 4, sweep)
+            planes(23, 31, 4, sweep)
+            planes(1, 5, 2, down0)
+            planes(11, 15, 2, down0)
+        else:
+            planes(1, 15, 2, down0)
 
         def start1(i):
             g = z_mean(y_pairs(r["S0"], i, 16), 0)
@@ -449,7 +460,8 @@
     for name in SEM:
         y_faces(name).wait_send()
         the_rest(name).wait_send()
-    field().wait_send()
+    field(0).wait_send()
+    field(1).wait_send()
     for cyc in range(CYCLES):
         ring = r["VF2"].at[cyc, 0:6]
         remote(ring, ring, S_SEM + cyc, 1, 0).wait_send()
@@ -458,7 +470,7 @@
 
 
 SEM = {"M": 0, "G": 2}
-V_SEM, S_SEM, C_SEM = 4, 5, 5 + CYCLES
+V_SEM, S_SEM, C_SEM = 4, 6, 6 + CYCLES
 CUT = {"M": 8, "G": 6, "VB": 7}
 FILL = {"M": "FM", "G": "FZ"}
 SPARE = {"M": "MS", "G": "GS"}

time: 45.6 us -> 45 us (0.987)
  Pallas kernels: 44.8 us -> 44.2 us
    pallas_call x1, Pallas kernels: 44.8 us -> 44.2 us  [local(): pl.pallas_call(functools.partial(kernel, nx, ny), out_shape=pltpu.VMEM(ri...]
where the time goes in v6:
time: 45 us; the launch traced here: 44.9 us
  Pallas kernels  44.2 us (98%)
  local copies, waits for them, and re-layouts  0.66 us (1%)
    pallas_call x1, Pallas kernels, local(): pl.pallas_call(functools.partial(kernel, nx, ny), out_shape=pltpu.VMEM(ri...  44.2 us

profile of v6, /device:TPU:1, one launch (start us, length us, event | category | flops | bytes accessed | tf_op | source)
XLA Modules:
  0.0 44.9 jit_solution(836428335825012934)
XLA Ops:
  0.0 44.2 %vcycles.1 = f32[16,16,128]{2,1,0:T(8,128)S(1)} custom-call(f32[16]{0:T(128)} %cond.1, f32[16,16,128]{2,1,0:T(8,128)} %g_hbm.1, s32[16,16,128]{2,1,0:T(8,128)} %m_hbm.1), custom_call_target="tpu_custom_call" | custom-call | tf_op jit(solution)/shard_map/vcycles/pallas_call | solution.py:500
  44.2 0.7 %copy.5 = f32[16,16,128]{2,1,0:T(8,128)} copy(f32[16,16,128]{2,1,0:T(8,128)S(1)} %vcycles.1) | data formatting | bytes 262144
